TPU v7x, 256 devices: a whole 4x4x8 slice. The times are simulated.
256 devices in a mesh: row: 16 (over y, x), col: 16 (over z, core).
Axes of the slice: x: 4, y: 4, z: 8, core: 2. Of those that a mesh axis runs over, the one named last changes fastest.
Arguments:
- flow_tiles: float32 [24576, 24576], P('row', 'col'), may hold values from 1 to 40
- anchor: float32 [48, 24576], P(None, 'row'), may hold values from 0.2 to 2
- destination: float32 [48, 24576], P(None, 'col'), may hold values from 0.2 to 2
Outputs:
- anchor_new: float32 [48, 24576], P(None, 'row')
- destination_new: float32 [48, 24576], P(None, 'col')
All inputs are finite; a program needn't handle non-finite values.
Results may differ from a plain program's by a relative error of at most 0.00011.
Values sent between devices are 32-bit elements; how exact they have to be, the bound alone decides.
No kernel may reach another device: no remote copies, remote signals or barrier semaphores. Data moves between devices by JAX's collectives and lax.ppermute only.
A program may use at most 64 MiB of HBM per device.

v0:
```python
import jax
import jax.numpy as jnp
from jax import lax
from jax.sharding import PartitionSpec as P

ITERS = 2


HIGH = lax.Precision.HIGHEST


def contract(left, right, dims):
    return lax.dot_general(
        left, right, (dims, ((), ())), precision=HIGH, preferred_element_type=jnp.float32
    )


def scale_anchor(flow_tiles, anchor, destination):
    rebuilt = contract(anchor, destination, ((0,), (0,)))
    ratios = flow_tiles / rebuilt
    partial_value = contract(destination, ratios, ((1,), (1,)))
    local_totals = jnp.sum(destination, axis=1)
    numerator, totals = lax.psum((partial_value, local_totals), "col")
    return anchor * numerator / totals[:, None]


def scale_destination(flow_tiles, anchor, destination):
    rebuilt = contract(anchor, destination, ((0,), (0,)))
    ratios = flow_tiles / rebuilt
    partial_value = contract(anchor, ratios, ((1,), (0,)))
    local_totals = jnp.sum(anchor, axis=1)
    numerator, totals = lax.psum((partial_value, local_totals), "row")
    return destination * numerator / totals[:, None]


def body(flow_tiles, anchor, destination):
    for sweep_index in range(ITERS):
        anchor = scale_anchor(flow_tiles, anchor, destination)
        destination = scale_destination(flow_tiles, anchor, destination)
    return (anchor, destination)


def solution(mesh):
    in_specs = (P("row", "col"), P(None, "row"), P(None, "col"))
    out_specs = (P(None, "row"), P(None, "col"))
    return jax.shard_map(body, mesh=mesh, in_specs=in_specs, out_specs=out_specs, check_vma=False)
```

profile of v0, /device:TPU:1, one launch (start us, length us, event | category | flops | bytes accessed | tf_op | source)
XLA Modules:
  0.0 495.3 jit_solution(17702453213014385037)
XLA Ops:
  7.2 8.7 %fusion.14 = f32[1536,1536]{1,0:T(8,128)S(1)} fusion(f32[48,1536]{1,0:T(8,128)} %param.4, f32[48,1536]{1,0:T(8,128)} %param.5), kind=kOutput, calls=%fused_computation.16 | convolution fusion | flops 1358954496 | bytes 10027008 | tf_op jit(solution)/shard_map/dot_general | solution.py:13
  16.0 10.8 %fusion.8 = f32[48,1536]{1,0:T(8,128)} fusion(f32[48,1536]{1,0:T(8,128)S(1)} %copy-done, f32[1536,1536]{1,0:T(8,128)S(1)} %copy-done.3, f32[1536,1536]{1,0:T(8,128)S(1)} %fusion.14), kind=kOutput, calls=%fused_computation.8 | convolution fusion | flops 1361313792 | bytes 19464192 | tf_op jit(solution)/shard_map/dot_general | solution.py:13
  26.8 0.0 all-reduce.7.cloned.1.call-start
  26.9 0.1 reduce_sum.36
  27.0 27.4 %psum.57 = f32[48]{0:T(128)S(1)} all-reduce(f32[48]{0:T(128)S(1)} %reduce_sum.36), channel_id=1, replica_groups=mesh['row'=16,'col'=16] {'col'}, use_global_device_ids=true, to_apply=%region_2.0 | all-reduce | flops 48 | bytes 384 | tf_op jit(solution)/shard_map/psum | solution.py:23
  54.4 82.8 %all-reduce.5.cloned.1.call-done = f32[48,1536]{1,0:T(8,128)} async-done(((f32[48,1536]{1,0:T(8,128)}), f32[48,1536]{1,0:T(8,128)}) %all-reduce.5.cloned.1.call-update) | async-done | bytes 294928 | tf_op jit(solution)/shard_map/psum | solution.py:23
  137.2 1.2 fusion.13
  138.4 7.5 %fusion.15 = f32[1536,1536]{1,0:T(8,128)S(1)} fusion(f32[48,1536]{1,0:T(8,128)S(1)} %get-tuple-element.7, f32[48,1536]{1,0:T(8,128)S(1)} %copy-done), kind=kOutput, calls=%fused_computation.17 | convolution fusion | flops 1358954496 | bytes 10027008 | tf_op jit(solution)/shard_map/dot_general | solution.py:13
  145.9 9.5 %fusion.4 = f32[48,1536]{1,0:T(8,128)} fusion(f32[48,1536]{1,0:T(8,128)S(1)} %get-tuple-element.7, f32[1536,1536]{1,0:T(8,128)} %param.3, f32[1536,1536]{1,0:T(8,128)S(1)} %fusion.15), kind=kOutput, calls=%fused_computation.4 | convolution fusion | flops 1361313792 | bytes 19464192 | tf_op jit(solution)/shard_map/dot_general | solution.py:13
  155.5 0.0 all-reduce.9.cloned.1.call-start
  155.5 33.3 %psum.59 = f32[48]{0:T(128)S(1)} all-reduce(f32[48]{0:T(128)S(1)} %get-tuple-element.6), channel_id=1, replica_groups=mesh['row'=16,'col'=16] {'row'}, use_global_device_ids=true, to_apply=%region_5.0 | all-reduce | flops 48 | bytes 384 | tf_op jit(solution)/shard_map/psum | solution.py:32
  188.8 58.9 %all-reduce.7.cloned.1.call-done = f32[48,1536]{1,0:T(8,128)} async-done(((f32[48,1536]{1,0:T(8,128)}), f32[48,1536]{1,0:T(8,128)}) %all-reduce.7.cloned.1.call-update) | async-done | bytes 294928 | tf_op jit(solution)/shard_map/psum | solution.py:32
  247.7 1.2 fusion.12
  248.9 7.5 %fusion.16 = f32[1536,1536]{1,0:T(8,128)S(1)} fusion(f32[48,1536]{1,0:T(8,128)S(1)} %get-tuple-element.7, f32[48,1536]{1,0:T(8,128)S(1)} %get-tuple-element.5), kind=kOutput, calls=%fused_computation.18 | convolution fusion | flops 1358954496 | bytes 10027008 | tf_op jit(solution)/shard_map/dot_general | solution.py:13
  256.4 12.2 %fusion.2 = f32[48,1536]{1,0:T(8,128)} fusion(f32[48,1536]{1,0:T(8,128)S(1)} %get-tuple-element.5, f32[1536,1536]{1,0:T(8,128)} %param.3, f32[1536,1536]{1,0:T(8,128)S(1)} %fusion.16), kind=kOutput, calls=%fused_computation.2 | convolution fusion | flops 1361313792 | bytes 19464192 | tf_op jit(solution)/shard_map/dot_general | solution.py:13
  268.6 0.0 all-reduce.11.cloned.1.call-start
  268.7 26.2 %psum.61 = f32[48]{0:T(128)S(1)} all-reduce(f32[48]{0:T(128)S(1)} %get-tuple-element.4), channel_id=1, replica_groups=mesh['row'=16,'col'=16] {'col'}, use_global_device_ids=true, to_apply=%region_8.0 | all-reduce | flops 48 | bytes 384 | tf_op jit(solution)/shard_map/psum | solution.py:23
  294.9 81.2 %all-reduce.9.cloned.1.call-done = f32[48,1536]{1,0:T(8,128)} async-done(((f32[48,1536]{1,0:T(8,128)}), f32[48,1536]{1,0:T(8,128)}) %all-reduce.9.cloned.1.call-update) | async-done | bytes 294928 | tf_op jit(solution)/shard_map/psum | solution.py:23
  376.0 1.2 fusion.11
  377.2 7.5 %fusion.17 = f32[1536,1536]{1,0:T(8,128)S(1)} fusion(f32[48,1536]{1,0:T(8,128)S(1)} %get-tuple-element.3, f32[48,1536]{1,0:T(8,128)S(1)} %get-tuple-element.5), kind=kOutput, calls=%fused_computation.19 | convolution fusion | flops 1358954496 | bytes 10027008 | tf_op jit(solution)/shard_map/dot_general | solution.py:13
  384.7 9.5 %fusion = f32[48,1536]{1,0:T(8,128)} fusion(f32[48,1536]{1,0:T(8,128)S(1)} %get-tuple-element.3, f32[1536,1536]{1,0:T(8,128)} %param.3, f32[1536,1536]{1,0:T(8,128)S(1)} %fusion.17), kind=kOutput, calls=%fused_computation | convolution fusion | flops 1361313792 | bytes 19464192 | tf_op jit(solution)/shard_map/dot_general | solution.py:13
  394.3 33.1 %psum.63 = f32[48]{0:T(128)S(1)} all-reduce(f32[48]{0:T(128)S(1)} %get-tuple-element.2), channel_id=1, replica_groups=mesh['row'=16,'col'=16] {'row'}, use_global_device_ids=true, to_apply=%region_11.0 | all-reduce | flops 48 | bytes 384 | tf_op jit(solution)/shard_map/psum | solution.py:32
  427.4 59.2 %all-reduce.11.cloned.1.call-done = f32[48,1536]{1,0:T(8,128)} async-done(((f32[48,1536]{1,0:T(8,128)}), f32[48,1536]{1,0:T(8,128)}) %all-reduce.11.cloned.1.call-update) | async-done | bytes 294928 | tf_op jit(solution)/shard_map/psum | solution.py:32
  486.6 1.8 multiply_divide_fusion
  (13 shorter events, 0.1 us)
Async XLA Ops:
  7.2 8.8 %copy-start = (f32[48,1536]{1,0:T(8,128)S(1)}, f32[48,1536]{1,0:T(8,128)}, u32[]{:S(2)}) copy-start(f32[48,1536]{1,0:T(8,128)} %param.5) | copy-start | bytes 884740
  7.2 130.1 %all-reduce.5.cloned.1.call-start = ((), (), s32[]{:S(2)}) async-start(), calls=%async_computation | async-start | bytes 589824 | tf_op jit(solution)/shard_map/psum | solution.py:23
  7.2 8.8 %copy-start.3 = (f32[1536,1536]{1,0:T(8,128)S(1)}, f32[1536,1536]{1,0:T(8,128)}, u32[]{:S(2)}) copy-start(f32[1536,1536]{1,0:T(8,128)} %param.3) | copy-start | bytes 28311556
  16.0 121.2 %copy-start.1 = (f32[48,1536]{1,0:T(8,128)S(1)}, f32[48,1536]{1,0:T(8,128)}, u32[]{:S(2)}) copy-start(f32[48,1536]{1,0:T(8,128)} %param.4) | copy-start | bytes 884740
  26.8 220.9 %all-reduce.7.cloned.1.call-start = ((), (), s32[]{:S(2)}) async-start(), calls=%async_computation.1 | async-start | bytes 589824 | tf_op jit(solution)/shard_map/psum | solution.py:32
  155.5 220.5 %all-reduce.9.cloned.1.call-start = ((), (), s32[]{:S(2)}) async-start(), calls=%async_computation.2 | async-start | bytes 589824 | tf_op jit(solution)/shard_map/psum | solution.py:23
  268.6 218.0 %all-reduce.11.cloned.1.call-start = ((), (), s32[]{:S(2)}) async-start(), calls=%async_computation.3 | async-start | bytes 589824 | tf_op jit(solution)/shard_map/psum | solution.py:32
  377.2 17.1 %copy-start.2 = (f32[48,1536]{1,0:T(8,128)}, f32[48,1536]{1,0:T(8,128)S(1)}, u32[]{:S(2)}) copy-start(f32[48,1536]{1,0:T(8,128)S(1)} %get-tuple-element.3) | copy-start | bytes 884740
Sparse Core Ops, SparseCore 0:
  26.9 110.2 all-reduce.4
  155.6 92.0 all-reduce.6
  268.7 107.2 all-reduce.8
  394.4 92.0 all-reduce.10
where the time goes:
time: 505 us; the launch traced here: 495 us
  waiting for transfers between devices  282 us (56%)
  blocking collectives  120 us (24%)
  matrix products  73.4 us (15%)
  between operations  14.3 us (3%)
  other arithmetic  5.38 us (1%)
    psum x2, waiting for transfers between devices, scale_anchor(): numerator, totals = lax.psum((partial_value, local_totals), 'col')  164 us
    psum x2, waiting for transfers between devices, scale_destination(): numerator, totals = lax.psum((partial_value, local_totals), 'row')  118 us
    dot_general x8, matrix products, contract(): lax.dot_general(left, right, (dims, ((), ())), precision=HIGH, preferred_...  73.4 us
    psum x2, blocking collectives, scale_destination(): numerator, totals = lax.psum((partial_value, local_totals), 'row')  66.4 us
    psum x2, blocking collectives, scale_anchor(): numerator, totals = lax.psum((partial_value, local_totals), 'col')  53.6 us
  transfers between devices with their start and end apart: 4, of which 4 were waited for; matrix products, arithmetic and copies ran while one was open for 0% of the time, Pallas kernels for 0%

commit v1 on v0

v1 whole, which is shorter than its diff:
```python
import functools

import jax
import jax.numpy as jnp
from jax import lax
from jax.experimental import pallas as pl
from jax.experimental.pallas import tpu as pltpu
from jax.sharding import PartitionSpec as P

ITERS = 2
RANK = 48
LANES = 128
COLS = 256
ROWS = 256

F32 = jnp.float32
BF16 = jnp.bfloat16

PIECE = 40


def split(x):
    high = x.astype(BF16)
    return high, (x - high.astype(F32)).astype(BF16)


def load_tile(ref, natural, part, tile, peers):
    if natural:
        return ref[part * peers : (part + 1) * peers, tile * LANES : (tile + 1) * LANES]
    tiles = 12
    return ref[pl.ds(part * tiles + tile, peers, stride=PIECE), :]


def store_pieces(out_ref, total, sums, peers):
    tiles = total.shape[1] // LANES
    parts = RANK // peers
    for part in range(parts):
        rows = slice(part * peers, (part + 1) * peers)
        for tile in range(tiles):
            out_ref[pl.ds(part * tiles + tile, peers, stride=PIECE), :] = total[
                rows, tile * LANES : (tile + 1) * LANES
            ]
        out_ref[pl.ds(parts * tiles + part, peers, stride=PIECE), :] = sums[rows]
    out_ref[pl.ds(parts * tiles + parts, peers, stride=PIECE), :] = jnp.zeros((peers, LANES), F32)


def half_kernel(
    kind, peers, nat_a, nat_d, emit_a, flow_hbm, a_ref, d_ref, out_ref, *rest
):
    if emit_a:
        a_out, *rest = rest
    a_f, a_t, a_cat, d_w, d_cat, acc, acc_t, *rest = rest
    flow, sem = rest
    zones_i, zones_j = flow.shape
    steps = zones_j // COLS
    parts = RANK // peers

    def fetch(step):
        at = pl.ds(step * COLS, COLS)
        return pltpu.make_async_copy(flow_hbm.at[:, at], flow.at[:, at], sem.at[step])

    for step in range(steps):
        fetch(step).start()

    sums = []
    for part in range(parts):
        total = None
        low = part * peers
        for tile in range(zones_j // LANES):
            at = slice(tile * LANES, (tile + 1) * LANES)
            x = load_tile(d_ref, nat_d, part, tile, peers)
            high, rest_x = split(x)
            for base in (0, 64):
                d_w[base + low : base + low + peers, at] = high
                d_w[128 + base + low : 128 + base + low + peers, at] = rest_x
            d_cat[low : low + peers, at] = high
            d_cat[RANK + low : RANK + low + peers, at] = rest_x
            if kind == "anchor":
                total = x if total is None else total + x
        for tile in range(zones_i // LANES):
            at = slice(tile * LANES, (tile + 1) * LANES)
            x = load_tile(a_ref, nat_a, part, tile, peers)
            high, rest_x = split(x)
            a_f[low : low + peers, at] = high.astype(F32)
            a_f[64 + low : 64 + low + peers, at] = rest_x.astype(F32)
            if kind == "destination":
                a_cat[low : low + peers, at] = high
                a_cat[RANK + low : RANK + low + peers, at] = rest_x
                total = x if total is None else total + x
            if emit_a:
                a_out[low : low + peers, at] = x
        sums.append(total)
    sums = jnp.concatenate(sums, axis=0)
    gap = jnp.zeros((16, zones_j), BF16)
    for base in (0, 64, 128, 192):
        d_w[base + RANK : base + 64, :] = gap
    gap = jnp.zeros((16, zones_i), F32)
    for base in (0, 64):
        a_f[base + RANK : base + 64, :] = gap
    for tile in range(zones_i // LANES):
        at = slice(tile * LANES, (tile + 1) * LANES)
        x = a_f[:, at].T.astype(BF16)
        a_t[at, :LANES] = x
        a_t[at, LANES:] = x

    if kind == "anchor":
        acc_t[...] = jnp.zeros_like(acc_t)

    def step_body(step, carry):
        fetch(step).wait()
        at = pl.ds(pl.multiple_of(step * COLS, COLS), COLS)
        weights = d_w[:, at]
        total = None
        for block in range(zones_i // ROWS):
            rows = slice(block * ROWS, (block + 1) * ROWS)
            rebuilt = jnp.dot(a_t[rows, :], weights, preferred_element_type=F32)
            piece = flow[rows, at]
            inverse = pl.reciprocal(rebuilt, approx=True)
            first = (piece * inverse).astype(BF16)
            second = ((piece - rebuilt * first.astype(F32)) * inverse).astype(BF16)
            if kind == "anchor":
                right = d_cat[:, at]
                dims = (((1,), (1,)), ((), ()))
                acc_t[rows, : 2 * RANK] += lax.dot_general(
                    first, right, dims, preferred_element_type=F32
                ) + lax.dot_general(second, right, dims, preferred_element_type=F32)
            else:
                left = a_cat[:, rows]
                term = jnp.dot(left, first, preferred_element_type=F32) + jnp.dot(
                    left, second, preferred_element_type=F32
                )
                total = term if total is None else total + term
        if kind == "destination":
            acc[:, at] = total[:RANK] + total[RANK:]
        return carry

    lax.fori_loop(0, steps, step_body, 0)

    if kind == "anchor":
        for tile in range(zones_i // LANES):
            at = slice(tile * LANES, (tile + 1) * LANES)
            x = acc_t[at, :].T
            acc[:, at] = x[:RANK] + x[RANK : 2 * RANK]
    store_pieces(out_ref, acc, sums, peers)


def half(kind, peers, flow, a, d, emit_a=False):
    zones_i, zones_j = flow.shape
    nat_a, nat_d = a.shape[0] == RANK, d.shape[0] == RANK
    out_shape = [jax.ShapeDtypeStruct((peers * PIECE, LANES), F32)]
    if emit_a:
        out_shape.append(jax.ShapeDtypeStruct((RANK, zones_i), F32))
    vmem = pl.BlockSpec(memory_space=pltpu.VMEM)
    own = [pltpu.VMEM((zones_i, zones_j), F32), pltpu.SemaphoreType.DMA((zones_j // COLS,))]
    out = pl.pallas_call(
        functools.partial(half_kernel, kind, peers, nat_a, nat_d, emit_a),
        out_shape=out_shape,
        in_specs=[pl.BlockSpec(memory_space=pl.ANY), vmem, vmem],
        out_specs=[vmem] * len(out_shape),
        scratch_shapes=[
            pltpu.VMEM((LANES, zones_i), F32),
            pltpu.VMEM((zones_i, 2 * LANES), BF16),
            pltpu.VMEM((2 * RANK, zones_i), BF16),
            pltpu.VMEM((2 * LANES, zones_j), BF16),
            pltpu.VMEM((2 * RANK, zones_j), BF16),
            pltpu.VMEM((RANK, zones_i), F32),
            pltpu.VMEM((zones_i, LANES), F32),
            *own,
        ],
        compiler_params=pltpu.CompilerParams(vmem_limit_bytes=32 * 2**20),
        name="half_" + kind,
    )(pltpu.with_memory_space_constraint(flow, pltpu.HBM), a, d)
    return out if emit_a else out[0]


def update_kernel(axis, peers, natural, got_ref, old_ref, out_ref, old):
    me = lax.axis_index(axis)
    parts = RANK // peers
    if natural:
        tiles = old_ref.shape[1] // LANES
        for part in range(parts):
            x = old_ref[part * peers : (part + 1) * peers, :]
            mine = lax.broadcasted_iota(jnp.int32, x.shape, 0) == me
            x = jnp.sum(jnp.where(mine, x, 0.0), axis=0, keepdims=True)
            for tile in range(tiles):
                row = part * tiles + tile
                old[row : row + 1, :] = x[:, tile * LANES : (tile + 1) * LANES]
        old[parts * tiles :, :] = jnp.zeros((PIECE - parts * tiles, LANES), F32)
        before = old[...]
    else:
        before = old_ref[pl.ds(pl.multiple_of(me * PIECE, 8), PIECE), :]
        tiles = 12
    total = got_ref[:PIECE, :]
    for peer in range(1, peers):
        total = total + got_ref[peer * PIECE : (peer + 1) * PIECE, :]
    row = lax.broadcasted_iota(jnp.int32, (PIECE, LANES), 0)
    norm = jnp.zeros((PIECE, LANES), F32)
    for part in range(parts):
        at = parts * tiles + part
        norm = jnp.where(row >= part * tiles, jnp.sum(total[at : at + 1, :]), norm)
    new = jnp.where(row < parts * tiles, before * total / norm, 0.0)
    for peer in range(peers):
        out_ref[peer * PIECE : (peer + 1) * PIECE, :] = new


def update(axis, peers, got, old):
    vmem = pl.BlockSpec(memory_space=pltpu.VMEM)
    return pl.pallas_call(
        functools.partial(update_kernel, axis, peers, old.shape[0] == RANK),
        out_shape=jax.ShapeDtypeStruct((peers * PIECE, LANES), F32),
        in_specs=[vmem, vmem],
        out_specs=vmem,
        scratch_shapes=[pltpu.VMEM((PIECE, LANES), F32)],
        compiler_params=pltpu.CompilerParams(vmem_limit_bytes=4 * 2**20),
        name="update",
    )(got, old)


def whole_kernel(peers, in_ref, out_ref):
    for part in range(RANK // peers):
        for tile in range(out_ref.shape[1] // LANES):
            out_ref[part * peers : (part + 1) * peers, tile * LANES : (tile + 1) * LANES] = load_tile(
                in_ref, False, part, tile, peers
            )


def whole(peers, pieces, zones):
    vmem = pl.BlockSpec(memory_space=pltpu.VMEM)
    return pl.pallas_call(
        functools.partial(whole_kernel, peers),
        out_shape=jax.ShapeDtypeStruct((RANK, zones), F32),
        in_specs=[vmem],
        out_specs=vmem,
        compiler_params=pltpu.CompilerParams(vmem_limit_bytes=4 * 2**20),
        name="whole",
    )(pieces)


def exchange(x, axis):
    return lax.all_to_all(x, axis, 0, 0, tiled=True)


def body(n_row, n_col, flow, anchor, destination):
    anchor_out = None
    for sweep in range(ITERS):
        sent = half("anchor", n_col, flow, anchor, destination)
        sent = update("col", n_col, exchange(sent, "col"), anchor)
        anchor = exchange(sent, "col")
        last = sweep == ITERS - 1
        sent = half("destination", n_row, flow, anchor, destination, emit_a=last)
        if last:
            sent, anchor_out = sent
        sent = update("row", n_row, exchange(sent, "row"), destination)
        destination = exchange(sent, "row")
    return anchor_out, whole(n_row, destination, flow.shape[1])


def solution(mesh):
    n_row, n_col = mesh.shape["row"], mesh.shape["col"]
    in_specs = (P("row", "col"), P(None, "row"), P(None, "col"))
    out_specs = (P(None, "row"), P(None, "col"))
    return jax.shard_map(
        functools.partial(body, n_row, n_col),
        mesh=mesh,
        in_specs=in_specs,
        out_specs=out_specs,
        check_vma=False,
    )
```

time: 505 us -> 159 us (0.31); the launches traced: 495 us -> 159 us
  waiting for transfers between devices: 282 us -> 0 us
  matrix products: 73.4 us -> 0 us
  Pallas kernels: 0 us -> 33.9 us
  between operations: 14.3 us -> 0.7 us
  other arithmetic: 5.38 us -> 0 us
    psum x4 -> x0, waiting for transfers between devices: 282 us -> none  [the longest x2 164 us: scale_anchor(): numerator, totals = lax.psum((partial_value, local_totals), 'col')]
    all_to_all x0 -> x8, blocking collectives: none -> 122 us  [exchange(): return lax.all_to_all(x, axis, 0, 0, tiled=True)]
    psum x4 -> x0, blocking collectives: 120 us -> none  [the longest x2 66.4 us: scale_destination(): numerator, totals = lax.psum((partial_value, local_totals), 'row')]
    dot_general x8 -> x0, matrix products: 73.4 us -> none  [contract(): lax.dot_general(left, right, (dims, ((), ())), precision=HIGH, preferred_...]
    pallas_call x0 -> x9, Pallas kernels: none -> 33.9 us  [the longest x4 32.5 us: half(): pl.pallas_call(functools.partial(half_kernel, kind, peers, nat_a, nat_d,...]
  transfers between devices with their start and end apart: 4 -> 0, of which waited for: 4 -> 0; matrix products, arithmetic and copies ran while one was open for 0% -> 0% of each run, Pallas kernels for 0% -> 0%
where the time goes in v1:
time: 159 us
  blocking collectives  122 us (77%)
  Pallas kernels  33.9 us (21%)
  local copies, waits for them, and re-layouts  1.92 us (1%)
    all_to_all x8, blocking collectives, exchange(): return lax.all_to_all(x, axis, 0, 0, tiled=True)  122 us
    pallas_call x4, Pallas kernels, half(): pl.pallas_call(functools.partial(half_kernel, kind, peers, nat_a, nat_d,...  32.5 us

profile of v1, /device:TPU:1, one launch (start us, length us, event | category | flops | bytes accessed | tf_op | source)
XLA Modules:
  0.0 158.6 jit_solution(13523696079043345106)
XLA Ops:
  0.6 0.0 copy-start
  0.6 1.0 copy-done
  1.6 0.0 copy-start.1
  1.6 1.0 copy-done.1
  2.6 10.1 %half_anchor.2 = f32[640,128]{1,0:T(8,128)S(1)} custom-call(f32[1536,1536]{1,0:T(8,128)} %flow_hbm.7, f32[48,1536]{1,0:T(8,128)S(1)} %copy-done.1, f32[48,1536]{1,0:T(8,128)S(1)} %copy-done), custom_call_target="tpu_custom_call" | custom-call | tf_op jit(solution)/shard_map/half_anchor/pallas_call | solution.py:155
  12.6 22.8 %all_to_all.88 = f32[16,40,128]{2,1,0:T(8,128)S(1)} all-to-all(f32[16,40,128]{2,1,0:T(8,128)S(1)} %bitcast.23), channel_id=1, replica_groups=mesh['row'=16,'col'=16] {'col'}, dimensions={0} | all-to-all | bytes 655360 | tf_op jit(solution)/shard_map/all_to_all | solution.py:240
  35.4 0.2 update.4
  35.6 15.8 %all_to_all.89 = f32[16,40,128]{2,1,0:T(8,128)S(1)} all-to-all(f32[16,40,128]{2,1,0:T(8,128)S(1)} %bitcast.32), channel_id=1, replica_groups=mesh['row'=16,'col'=16] {'col'}, dimensions={0} | all-to-all | bytes 655360 | tf_op jit(solution)/shard_map/all_to_all | solution.py:240
  51.3 6.2 %half_destination.2 = f32[640,128]{1,0:T(8,128)S(1)} custom-call(f32[1536,1536]{1,0:T(8,128)} %flow_hbm.7, f32[640,128]{1,0:T(8,128)S(1)} %bitcast.19, f32[48,1536]{1,0:T(8,128)S(1)} %copy-done), custom_call_target="tpu_custom_call" | custom-call | tf_op jit(solution)/shard_map/half_destination/pallas_call | solution.py:155
  57.5 16.0 %all_to_all.90 = f32[16,40,128]{2,1,0:T(8,128)S(1)} all-to-all(f32[16,40,128]{2,1,0:T(8,128)S(1)} %bitcast.24), channel_id=1, replica_groups=mesh['row'=16,'col'=16] {'row'}, dimensions={0} | all-to-all | bytes 655360 | tf_op jit(solution)/shard_map/all_to_all | solution.py:240
  73.5 0.2 update.5
  73.6 11.2 %all_to_all.91 = f32[16,40,128]{2,1,0:T(8,128)S(1)} all-to-all(f32[16,40,128]{2,1,0:T(8,128)S(1)} %bitcast.34), channel_id=1, replica_groups=mesh['row'=16,'col'=16] {'row'}, dimensions={0} | all-to-all | bytes 655360 | tf_op jit(solution)/shard_map/all_to_all | solution.py:240
  84.8 10.1 %half_anchor.3 = f32[640,128]{1,0:T(8,128)S(1)} custom-call(f32[1536,1536]{1,0:T(8,128)} %flow_hbm.7, f32[640,128]{1,0:T(8,128)S(1)} %bitcast.20, f32[640,128]{1,0:T(8,128)S(1)} %bitcast.16), custom_call_target="tpu_custom_call" | custom-call | tf_op jit(solution)/shard_map/half_anchor/pallas_call | solution.py:155
  94.9 17.7 %all_to_all.92 = f32[16,40,128]{2,1,0:T(8,128)S(1)} all-to-all(f32[16,40,128]{2,1,0:T(8,128)S(1)} %bitcast.25), channel_id=1, replica_groups=mesh['row'=16,'col'=16] {'col'}, dimensions={0} | all-to-all | bytes 655360 | tf_op jit(solution)/shard_map/all_to_all | solution.py:240
  112.5 0.2 update.6
  112.7 15.5 %all_to_all.93 = f32[16,40,128]{2,1,0:T(8,128)S(1)} all-to-all(f32[16,40,128]{2,1,0:T(8,128)S(1)} %bitcast.28), channel_id=1, replica_groups=mesh['row'=16,'col'=16] {'col'}, dimensions={0} | all-to-all | bytes 655360 | tf_op jit(solution)/shard_map/all_to_all | solution.py:240
  128.2 6.2 %half_destination.3 = (f32[640,128]{1,0:T(8,128)S(1)}, f32[48,1536]{1,0:T(8,128)}) custom-call(f32[1536,1536]{1,0:T(8,128)} %flow_hbm.7, f32[640,128]{1,0:T(8,128)S(1)} %bitcast.22, f32[640,128]{1,0:T(8,128)S(1)} %bitcast.17), custom_call_target="tpu_custom_call" | custom-call | tf_op jit(solution)/shard_map/half_destination/pallas_call | solution.py:155
  134.5 12.0 %all_to_all.94 = f32[16,40,128]{2,1,0:T(8,128)S(1)} all-to-all(f32[16,40,128]{2,1,0:T(8,128)S(1)} %bitcast.35), channel_id=1, replica_groups=mesh['row'=16,'col'=16] {'row'}, dimensions={0} | all-to-all | bytes 655360 | tf_op jit(solution)/shard_map/all_to_all | solution.py:240
  146.5 0.2 update.7
  146.7 11.2 %all_to_all.95 = f32[16,40,128]{2,1,0:T(8,128)S(1)} all-to-all(f32[16,40,128]{2,1,0:T(8,128)S(1)} %bitcast.30), channel_id=1, replica_groups=mesh['row'=16,'col'=16] {'row'}, dimensions={0} | all-to-all | bytes 655360 | tf_op jit(solution)/shard_map/all_to_all | solution.py:240
  157.9 0.8 whole.1
Async XLA Ops:
  0.6 1.0 copy-start
  1.6 1.0 copy-start.1

commit v2 on v1

v2 whole, which is shorter than its diff:
```python
import functools

import jax
import jax.numpy as jnp
from jax import lax
from jax.experimental import pallas as pl
from jax.experimental.pallas import tpu as pltpu
from jax.sharding import PartitionSpec as P

ITERS = 2
RANK = 48
LANES = 128
COLS = 256
ROWS = 256

F32 = jnp.float32
BF16 = jnp.bfloat16

PIECE = 40


def split(x):
    high = x.astype(BF16)
    return high, (x - high.astype(F32)).astype(BF16)


def load_tile(ref, natural, part, tile, peers):
    if natural:
        return ref[part * peers : (part + 1) * peers, tile * LANES : (tile + 1) * LANES]
    tiles = 12
    return ref[pl.ds(part * tiles + tile, peers, stride=PIECE), :]


def store_pieces(out_ref, total, sums, peers):
    tiles = total.shape[1] // LANES
    parts = RANK // peers
    for part in range(parts):
        rows = slice(part * peers, (part + 1) * peers)
        for tile in range(tiles):
            out_ref[pl.ds(part * tiles + tile, peers, stride=PIECE), :] = total[
                rows, tile * LANES : (tile + 1) * LANES
            ]
        out_ref[pl.ds(parts * tiles + part, peers, stride=PIECE), :] = sums[rows]
    out_ref[pl.ds(parts * tiles + parts, peers, stride=PIECE), :] = jnp.zeros((peers, LANES), F32)


def half_kernel(kind, peers, nat_u, nat_v, emit_v, first, flow_in, u_ref, v_ref, out_ref, *rest):
    rest = list(rest)
    v_out = rest.pop(0) if emit_v else None
    flow = rest.pop(0) if first else flow_in
    v_f, v_t, v_cat, u_w, acc, *sem = rest
    zones_u, zones_v = u_w.shape[1], v_t.shape[0]
    steps = zones_u // COLS
    parts = RANK // peers

    def fetch(step):
        at = pl.ds(step * COLS, COLS)
        where = (at, slice(None)) if kind == "anchor" else (slice(None), at)
        return pltpu.make_async_copy(flow_in.at[where], flow.at[where], sem[0].at[step])

    if first:
        for step in range(steps):
            fetch(step).start()

    sums = []
    for part in range(parts):
        total = None
        low = part * peers
        for tile in range(zones_u // LANES):
            at = slice(tile * LANES, (tile + 1) * LANES)
            high, low_term = split(load_tile(u_ref, nat_u, part, tile, peers))
            for base in (0, 64):
                u_w[base + low : base + low + peers, at] = high
                u_w[128 + base + low : 128 + base + low + peers, at] = low_term
        for tile in range(zones_v // LANES):
            at = slice(tile * LANES, (tile + 1) * LANES)
            x = load_tile(v_ref, nat_v, part, tile, peers)
            high, low_term = split(x)
            v_f[low : low + peers, at] = high.astype(F32)
            v_f[64 + low : 64 + low + peers, at] = low_term.astype(F32)
            v_cat[low : low + peers, at] = high
            v_cat[RANK + low : RANK + low + peers, at] = low_term
            total = x if total is None else total + x
            if emit_v:
                v_out[low : low + peers, at] = x
        sums.append(total)
    sums = jnp.concatenate(sums, axis=0)
    gap = jnp.zeros((16, zones_u), BF16)
    for base in (0, 64, 128, 192):
        u_w[base + RANK : base + 64, :] = gap
    gap = jnp.zeros((16, zones_v), F32)
    for base in (0, 64):
        v_f[base + RANK : base + 64, :] = gap
    for tile in range(zones_v // LANES):
        at = slice(tile * LANES, (tile + 1) * LANES)
        x = v_f[:, at].T.astype(BF16)
        v_t[at, :LANES] = x
        v_t[at, LANES:] = x

    def step_body(step, carry):
        if first:
            fetch(step).wait()
        at = pl.ds(pl.multiple_of(step * COLS, COLS), COLS)
        weights = u_w[:, at]
        total = None
        for block in range(zones_v // ROWS):
            rows = slice(block * ROWS, (block + 1) * ROWS)
            rebuilt = jnp.dot(v_t[rows, :], weights, preferred_element_type=F32)
            piece = flow[at, rows].T if kind == "anchor" else flow[rows, at]
            inverse = pl.reciprocal(rebuilt, approx=True)
            head = (piece * inverse).astype(BF16)
            tail = ((piece - rebuilt * head.astype(F32)) * inverse).astype(BF16)
            left = v_cat[:, rows]
            term = jnp.dot(left, head, preferred_element_type=F32)
            term += jnp.dot(left, tail, preferred_element_type=F32)
            total = term if total is None else total + term
        acc[:, at] = total[:RANK] + total[RANK:]
        return carry

    lax.fori_loop(0, steps, step_body, 0)
    store_pieces(out_ref, acc, sums, peers)


def half(kind, peers, flow, u, v, emit_v=False, first=False):
    zones_u, zones_v = flow.shape if kind == "anchor" else flow.shape[::-1]
    nat_u, nat_v = u.shape[0] == RANK, v.shape[0] == RANK
    vmem = pl.BlockSpec(memory_space=pltpu.VMEM)
    out_shape = [jax.ShapeDtypeStruct((peers * PIECE, LANES), F32)]
    if emit_v:
        out_shape.append(jax.ShapeDtypeStruct((RANK, zones_v), F32))
    if first:
        out_shape.append(pltpu.VMEM(flow.shape, F32))
        flow = pltpu.with_memory_space_constraint(flow, pltpu.HBM)
    return pl.pallas_call(
        functools.partial(half_kernel, kind, peers, nat_u, nat_v, emit_v, first),
        out_shape=out_shape,
        in_specs=[pl.BlockSpec(memory_space=pl.ANY) if first else vmem, vmem, vmem],
        out_specs=[vmem] * len(out_shape),
        scratch_shapes=[
            pltpu.VMEM((LANES, zones_v), F32),
            pltpu.VMEM((zones_v, 2 * LANES), BF16),
            pltpu.VMEM((2 * RANK, zones_v), BF16),
            pltpu.VMEM((2 * LANES, zones_u), BF16),
            pltpu.VMEM((RANK, zones_u), F32),
            *([pltpu.SemaphoreType.DMA((zones_u // COLS,))] if first else []),
        ],
        compiler_params=pltpu.CompilerParams(vmem_limit_bytes=30 * 2**20),
        name="half_" + kind,
    )(flow, u, v)


def update_kernel(axis, peers, natural, got_ref, old_ref, out_ref, old):
    me = lax.axis_index(axis)
    parts = RANK // peers
    if natural:
        tiles = old_ref.shape[1] // LANES
        for part in range(parts):
            x = old_ref[part * peers : (part + 1) * peers, :]
            mine = lax.broadcasted_iota(jnp.int32, x.shape, 0) == me
            x = jnp.sum(jnp.where(mine, x, 0.0), axis=0, keepdims=True)
            for tile in range(tiles):
                row = part * tiles + tile
                old[row : row + 1, :] = x[:, tile * LANES : (tile + 1) * LANES]
        old[parts * tiles :, :] = jnp.zeros((PIECE - parts * tiles, LANES), F32)
        before = old[...]
    else:
        before = old_ref[pl.ds(pl.multiple_of(me * PIECE, 8), PIECE), :]
        tiles = 12
    total = got_ref[:PIECE, :]
    for peer in range(1, peers):
        total = total + got_ref[peer * PIECE : (peer + 1) * PIECE, :]
    row = lax.broadcasted_iota(jnp.int32, (PIECE, LANES), 0)
    norm = jnp.zeros((PIECE, LANES), F32)
    for part in range(parts):
        at = parts * tiles + part
        norm = jnp.where(row >= part * tiles, jnp.sum(total[at : at + 1, :]), norm)
    new = jnp.where(row < parts * tiles, before * total / norm, 0.0)
    for peer in range(peers):
        out_ref[peer * PIECE : (peer + 1) * PIECE, :] = new


def update(axis, peers, got, old):
    vmem = pl.BlockSpec(memory_space=pltpu.VMEM)
    return pl.pallas_call(
        functools.partial(update_kernel, axis, peers, old.shape[0] == RANK),
        out_shape=jax.ShapeDtypeStruct((peers * PIECE, LANES), F32),
        in_specs=[vmem, vmem],
        out_specs=vmem,
        scratch_shapes=[pltpu.VMEM((PIECE, LANES), F32)],
        compiler_params=pltpu.CompilerParams(vmem_limit_bytes=4 * 2**20),
        name="update",
    )(got, old)


def whole_kernel(peers, in_ref, out_ref):
    for part in range(RANK // peers):
        for tile in range(out_ref.shape[1] // LANES):
            out_ref[part * peers : (part + 1) * peers, tile * LANES : (tile + 1) * LANES] = load_tile(
                in_ref, False, part, tile, peers
            )


def whole(peers, pieces, zones):
    vmem = pl.BlockSpec(memory_space=pltpu.VMEM)
    return pl.pallas_call(
        functools.partial(whole_kernel, peers),
        out_shape=jax.ShapeDtypeStruct((RANK, zones), F32),
        in_specs=[vmem],
        out_specs=vmem,
        compiler_params=pltpu.CompilerParams(vmem_limit_bytes=4 * 2**20),
        name="whole",
    )(pieces)


def exchange(x, axis):
    return lax.all_to_all(x, axis, 0, 0, tiled=True)


def body(n_row, n_col, flow, anchor, destination):
    anchor_out = None
    for sweep in range(ITERS):
        if sweep == 0:
            sent, flow = half("anchor", n_col, flow, anchor, destination, first=True)
        else:
            (sent,) = half("anchor", n_col, flow, anchor, destination)
        sent = update("col", n_col, exchange(sent, "col"), anchor)
        anchor = exchange(sent, "col")
        last = sweep == ITERS - 1
        sent, *rest = half("destination", n_row, flow, destination, anchor, emit_v=last)
        if last:
            (anchor_out,) = rest
        sent = update("row", n_row, exchange(sent, "row"), destination)
        destination = exchange(sent, "row")
    return anchor_out, whole(n_row, destination, flow.shape[1])


def solution(mesh):
    n_row, n_col = mesh.shape["row"], mesh.shape["col"]
    in_specs = (P("row", "col"), P(None, "row"), P(None, "col"))
    out_specs = (P(None, "row"), P(None, "col"))
    return jax.shard_map(
        functools.partial(body, n_row, n_col),
        mesh=mesh,
        in_specs=in_specs,
        out_specs=out_specs,
        check_vma=False,
    )
```

time: 159 us -> 148 us (0.931)
  Pallas kernels: 33.9 us -> 22.6 us
    pallas_call x4, Pallas kernels: 32.5 us -> 21.2 us  [half(): pl.pallas_call(functools.partial(half_kernel, kind, peers, nat_u, nat_v,...]
where the time goes in v2:
time: 148 us; the launch traced here: 147 us
  blocking collectives  122 us (82%)
  Pallas kernels  22.6 us (15%)
  local copies, waits for them, and re-layouts  1.92 us (1%)
    all_to_all x8, blocking collectives, exchange(): return lax.all_to_all(x, axis, 0, 0, tiled=True)  122 us
    pallas_call x4, Pallas kernels, half(): pl.pallas_call(functools.partial(half_kernel, kind, peers, nat_u, nat_v,...  21.2 us

profile of v2, /device:TPU:1, one launch (start us, length us, event | category | flops | bytes accessed | tf_op | source)
XLA Modules:
  0.0 147.3 jit_solution(10120069271004863927)
XLA Ops:
  0.6 0.0 copy-start
  0.6 1.0 copy-done
  1.6 0.0 copy-start.2
  1.6 1.0 copy-done.2
  2.6 0.0 copy-start.1
  2.6 6.2 %half_anchor.2 = (f32[640,128]{1,0:T(8,128)S(1)}, f32[1536,1536]{1,0:T(8,128)S(1)}) custom-call(f32[1536,1536]{1,0:T(8,128)} %flow_in.1, f32[48,1536]{1,0:T(8,128)S(1)} %copy-done.2, f32[48,1536]{1,0:T(8,128)S(1)} %copy-done), custom_call_target="tpu_custom_call" | custom-call | tf_op jit(solution)/shard_map/half_anchor/pallas_call | solution.py:134
  8.8 22.7 %all_to_all.88 = f32[16,40,128]{2,1,0:T(8,128)S(1)} all-to-all(f32[16,40,128]{2,1,0:T(8,128)S(1)} %bitcast.35), channel_id=1, replica_groups=mesh['row'=16,'col'=16] {'col'}, dimensions={0} | all-to-all | bytes 655360 | tf_op jit(solution)/shard_map/all_to_all | solution.py:216
  31.5 0.2 update.4
  31.7 15.8 %all_to_all.89 = f32[16,40,128]{2,1,0:T(8,128)S(1)} all-to-all(f32[16,40,128]{2,1,0:T(8,128)S(1)} %bitcast.31), channel_id=1, replica_groups=mesh['row'=16,'col'=16] {'col'}, dimensions={0} | all-to-all | bytes 655360 | tf_op jit(solution)/shard_map/all_to_all | solution.py:216
  47.5 0.0 copy-done.1
  47.5 5.0 %half_destination.2 = f32[640,128]{1,0:T(8,128)S(1)} custom-call(f32[1536,1536]{1,0:T(8,128)S(1)} %get-tuple-element.6.flow_in, f32[48,1536]{1,0:T(8,128)S(1)} %copy-done.1, f32[640,128]{1,0:T(8,128)S(1)} %bitcast.19), custom_call_target="tpu_custom_call" | custom-call | tf_op jit(solution)/shard_map/half_destination/pallas_call | solution.py:134
  52.4 16.0 %all_to_all.90 = f32[16,40,128]{2,1,0:T(8,128)S(1)} all-to-all(f32[16,40,128]{2,1,0:T(8,128)S(1)} %bitcast.23), channel_id=1, replica_groups=mesh['row'=16,'col'=16] {'row'}, dimensions={0} | all-to-all | bytes 655360 | tf_op jit(solution)/shard_map/all_to_all | solution.py:216
  68.4 0.2 update.5
  68.6 11.2 %all_to_all.91 = f32[16,40,128]{2,1,0:T(8,128)S(1)} all-to-all(f32[16,40,128]{2,1,0:T(8,128)S(1)} %bitcast.33), channel_id=1, replica_groups=mesh['row'=16,'col'=16] {'row'}, dimensions={0} | all-to-all | bytes 655360 | tf_op jit(solution)/shard_map/all_to_all | solution.py:216
  79.8 5.0 %half_anchor.3 = f32[640,128]{1,0:T(8,128)S(1)} custom-call(f32[1536,1536]{1,0:T(8,128)S(1)} %get-tuple-element.6.flow_in, f32[640,128]{1,0:T(8,128)S(1)} %bitcast.20, f32[640,128]{1,0:T(8,128)S(1)} %bitcast.16), custom_call_target="tpu_custom_call" | custom-call | tf_op jit(solution)/shard_map/half_anchor/pallas_call | solution.py:134
  84.8 17.7 %all_to_all.92 = f32[16,40,128]{2,1,0:T(8,128)S(1)} all-to-all(f32[16,40,128]{2,1,0:T(8,128)S(1)} %bitcast.24), channel_id=1, replica_groups=mesh['row'=16,'col'=16] {'col'}, dimensions={0} | all-to-all | bytes 655360 | tf_op jit(solution)/shard_map/all_to_all | solution.py:216
  102.4 0.2 update.6
  102.6 15.5 %all_to_all.93 = f32[16,40,128]{2,1,0:T(8,128)S(1)} all-to-all(f32[16,40,128]{2,1,0:T(8,128)S(1)} %bitcast.27), channel_id=1, replica_groups=mesh['row'=16,'col'=16] {'col'}, dimensions={0} | all-to-all | bytes 655360 | tf_op jit(solution)/shard_map/all_to_all | solution.py:216
  118.1 5.0 %half_destination.3 = (f32[640,128]{1,0:T(8,128)S(1)}, f32[48,1536]{1,0:T(8,128)}) custom-call(f32[1536,1536]{1,0:T(8,128)S(1)} %get-tuple-element.6.flow_in, f32[640,128]{1,0:T(8,128)S(1)} %bitcast.17, f32[640,128]{1,0:T(8,128)S(1)} %bitcast.22), custom_call_target="tpu_custom_call" | custom-call | tf_op jit(solution)/shard_map/half_destination/pallas_call | solution.py:134
  123.1 12.1 %all_to_all.94 = f32[16,40,128]{2,1,0:T(8,128)S(1)} all-to-all(f32[16,40,128]{2,1,0:T(8,128)S(1)} %bitcast.34), channel_id=1, replica_groups=mesh['row'=16,'col'=16] {'row'}, dimensions={0} | all-to-all | bytes 655360 | tf_op jit(solution)/shard_map/all_to_all | solution.py:216
  135.2 0.2 update.7
  135.3 11.2 %all_to_all.95 = f32[16,40,128]{2,1,0:T(8,128)S(1)} all-to-all(f32[16,40,128]{2,1,0:T(8,128)S(1)} %bitcast.29), channel_id=1, replica_groups=mesh['row'=16,'col'=16] {'row'}, dimensions={0} | all-to-all | bytes 655360 | tf_op jit(solution)/shard_map/all_to_all | solution.py:216
  146.5 0.8 whole.1
Async XLA Ops:
  0.6 1.0 copy-start
  1.6 1.0 copy-start.2
  2.6 44.9 %copy-start.1 = (f32[48,1536]{1,0:T(8,128)S(1)}, f32[48,1536]{1,0:T(8,128)}, u32[]{:S(2)}) copy-start(f32[48,1536]{1,0:T(8,128)} %old_ref.3) | copy-start | bytes 884740

commit v3 on v2

v3 whole, which is shorter than its diff:
```python
import functools

import jax
import jax.numpy as jnp
from jax import lax
from jax.experimental import pallas as pl
from jax.experimental.pallas import tpu as pltpu
from jax.sharding import PartitionSpec as P

ITERS = 2
RANK = 48
LANES = 128
COLS = 256
ROWS = 256

F32 = jnp.float32
BF16 = jnp.bfloat16

PART = 16
PARTS = RANK // PART

PIECE = 40
TILES = 12
VMEM = pl.BlockSpec(memory_space=pltpu.VMEM)


def split(x):
    high = x.astype(BF16)
    return high, (x - high.astype(F32)).astype(BF16)


def swap(core, mine, other):
    return jnp.where(core == 0, mine, other), jnp.where(core == 0, other, mine)


def load_tile(refs, core, part, tile):
    if refs[0].shape[0] == RANK:
        return refs[0][part * PART : (part + 1) * PART, tile * LANES : (tile + 1) * LANES]
    row = part * TILES + tile
    if len(refs) == 1:
        return refs[0][pl.ds(row, PART, stride=PIECE), :]
    half_part = [ref[pl.ds(row, PART // 2, stride=PIECE), :] for ref in refs]
    return jnp.concatenate(swap(core, *half_part), axis=0)


def store_rows(refs, core, row, x):
    if len(refs) == 1:
        refs[0][pl.ds(row, PART, stride=PIECE), :] = x
    else:
        for ref, y in zip(refs, swap(core, x[: PART // 2], x[PART // 2 :])):
            ref[pl.ds(row, PART // 2, stride=PIECE), :] = y


def half_kernel(kind, n_u, n_v, n_out, emit_v, first, *refs):
    refs = list(refs)
    take = lambda n: [refs.pop(0) for _ in range(n)]
    (flow_in,), u_refs, v_refs, out_refs = take(1), take(n_u), take(n_v), take(n_out)
    (v_out,) = take(1) if emit_v else (None,)
    (flow,) = take(1) if first else (flow_in,)
    v_f, v_t, v_cat, u_w, acc = take(5)
    zones_u, zones_v = u_w.shape[1], v_t.shape[0]
    steps = zones_u // COLS
    core = lax.rem(lax.axis_index("col"), 2)

    def fetch(step):
        at = pl.ds(step * COLS, COLS)
        where = (at, slice(None)) if kind == "anchor" else (slice(None), at)
        return pltpu.make_async_copy(flow_in.at[where], flow.at[where], sem.at[step])

    if first:
        u_buf, v_buf, sem, factor_sem = refs
        copies = [
            pltpu.make_async_copy(u_refs[0], u_buf, factor_sem.at[0]),
            pltpu.make_async_copy(v_refs[0], v_buf, factor_sem.at[1]),
        ]
        for copy in copies:
            copy.start()
        fetch(0).start()
        for copy in copies:
            copy.wait()
        fetch(1).start()
        u_refs, v_refs = [u_buf], [v_buf]

    sums = []
    for part in range(PARTS):
        total = None
        low = part * PART
        for tile in range(zones_u // LANES):
            at = slice(tile * LANES, (tile + 1) * LANES)
            high, low_term = split(load_tile(u_refs, core, part, tile))
            for base in (0, 64):
                u_w[base + low : base + low + PART, at] = high
                u_w[128 + base + low : 128 + base + low + PART, at] = low_term
        for tile in range(zones_v // LANES):
            at = slice(tile * LANES, (tile + 1) * LANES)
            x = load_tile(v_refs, core, part, tile)
            high, low_term = split(x)
            v_f[low : low + PART, at] = high.astype(F32)
            v_f[64 + low : 64 + low + PART, at] = low_term.astype(F32)
            v_cat[low : low + PART, at] = high
            v_cat[RANK + low : RANK + low + PART, at] = low_term
            total = x if total is None else total + x
            if emit_v:
                v_out[low : low + PART, at] = x
        sums.append(total)
    gap = jnp.zeros((16, zones_u), BF16)
    for base in (0, 64, 128, 192):
        u_w[base + RANK : base + 64, :] = gap
    gap = jnp.zeros((16, zones_v), F32)
    for base in (0, 64):
        v_f[base + RANK : base + 64, :] = gap
    for tile in range(zones_v // LANES):
        at = slice(tile * LANES, (tile + 1) * LANES)
        x = v_f[:, at].T.astype(BF16)
        v_t[at, :LANES] = x
        v_t[at, LANES:] = x

    def step_body(step, carry):
        if first:
            fetch(step).wait()

            @pl.when(step + 2 < steps)
            def _():
                fetch(step + 2).start()

        at = pl.ds(pl.multiple_of(step * COLS, COLS), COLS)
        weights = u_w[:, at]
        total = None
        for block in range(zones_v // ROWS):
            rows = slice(block * ROWS, (block + 1) * ROWS)
            rebuilt = jnp.dot(v_t[rows, :], weights, preferred_element_type=F32)
            piece = flow[at, rows].T if kind == "anchor" else flow[rows, at]
            inverse = pl.reciprocal(rebuilt, approx=True)
            head = (piece * inverse).astype(BF16)
            tail = ((piece - rebuilt * head.astype(F32)) * inverse).astype(BF16)
            left = v_cat[:, rows]
            term = jnp.dot(left, head, preferred_element_type=F32)
            term += jnp.dot(left, tail, preferred_element_type=F32)
            total = term if total is None else total + term
        acc[:, at] = total[:RANK] + total[RANK:]
        return carry

    lax.fori_loop(0, steps, step_body, 0)

    for part in range(PARTS):
        ranks = slice(part * PART, (part + 1) * PART)
        for tile in range(TILES):
            x = acc[ranks, tile * LANES : (tile + 1) * LANES]
            store_rows(out_refs, core, part * TILES + tile, x)
        store_rows(out_refs, core, PARTS * TILES + part, sums[part])
    store_rows(out_refs, core, PARTS * TILES + PARTS, jnp.zeros((PART, LANES), F32))


def half(kind, flow, u, v, emit_v=False, first=False):
    zones_u, zones_v = flow.shape if kind == "anchor" else flow.shape[::-1]
    n_out = 2 if kind == "anchor" else 1
    out_shape = [jax.ShapeDtypeStruct((PART // n_out * PIECE, LANES), F32)] * n_out
    if emit_v:
        out_shape.append(jax.ShapeDtypeStruct((RANK, zones_v), F32))
    scratch = [
        pltpu.VMEM((LANES, zones_v), F32),
        pltpu.VMEM((zones_v, 2 * LANES), BF16),
        pltpu.VMEM((2 * RANK, zones_v), BF16),
        pltpu.VMEM((2 * LANES, zones_u), BF16),
        pltpu.VMEM((RANK, zones_u), F32),
    ]
    operands = [flow, *u, *v]
    if first:
        out_shape.append(pltpu.VMEM(flow.shape, F32))
        operands = [pltpu.with_memory_space_constraint(x, pltpu.HBM) for x in operands]
        scratch += [
            pltpu.VMEM((RANK, zones_u), F32),
            pltpu.VMEM((RANK, zones_v), F32),
            pltpu.SemaphoreType.DMA((zones_u // COLS,)),
            pltpu.SemaphoreType.DMA((2,)),
        ]
    return pl.pallas_call(
        functools.partial(half_kernel, kind, len(u), len(v), n_out, emit_v, first),
        out_shape=out_shape,
        in_specs=[pl.BlockSpec(memory_space=pl.ANY) if first else VMEM] * len(operands),
        out_specs=[VMEM] * len(out_shape),
        scratch_shapes=scratch,
        compiler_params=pltpu.CompilerParams(vmem_limit_bytes=30 * 2**20),
        name="half_" + kind,
    )(*operands)


def update_kernel(axis, peers, got_ref, old_ref, out_ref, old):
    me = lax.axis_index(axis)
    if axis == "col":
        slot, core = me // 2, lax.rem(me, 2)
        me = core * (PART // 2) + slot
    else:
        slot = me
    if old_ref.shape[0] == RANK:
        for part in range(PARTS):
            x = old_ref[part * PART : (part + 1) * PART, :]
            mine = lax.broadcasted_iota(jnp.int32, x.shape, 0) == me
            x = jnp.sum(jnp.where(mine, x, 0.0), axis=0, keepdims=True)
            for tile in range(TILES):
                row = part * TILES + tile
                old[row : row + 1, :] = x[:, tile * LANES : (tile + 1) * LANES]
        old[PARTS * TILES :, :] = jnp.zeros((PIECE - PARTS * TILES, LANES), F32)
        before = old[...]
    else:
        before = old_ref[pl.ds(pl.multiple_of(slot * PIECE, 8), PIECE), :]
    total = got_ref[:PIECE, :]
    for peer in range(1, peers):
        total = total + got_ref[peer * PIECE : (peer + 1) * PIECE, :]
    row = lax.broadcasted_iota(jnp.int32, (PIECE, LANES), 0)
    norm = jnp.zeros((PIECE, LANES), F32)
    for part in range(PARTS):
        at = PARTS * TILES + part
        norm = jnp.where(row >= part * TILES, jnp.sum(total[at : at + 1, :]), norm)
    new = jnp.where(row < PARTS * TILES, before * total / norm, 0.0)
    for peer in range(peers):
        out_ref[peer * PIECE : (peer + 1) * PIECE, :] = new


def update(axis, got, old):
    return pl.pallas_call(
        functools.partial(update_kernel, axis, got.shape[0] // PIECE),
        out_shape=jax.ShapeDtypeStruct(got.shape, F32),
        in_specs=[VMEM, VMEM],
        out_specs=VMEM,
        scratch_shapes=[pltpu.VMEM((PIECE, LANES), F32)],
        compiler_params=pltpu.CompilerParams(vmem_limit_bytes=4 * 2**20),
        name="update",
    )(got, old[0])


def whole_kernel(in_ref, out_ref):
    for part in range(PARTS):
        for tile in range(TILES):
            at = slice(tile * LANES, (tile + 1) * LANES)
            out_ref[part * PART : (part + 1) * PART, at] = load_tile([in_ref], None, part, tile)


def whole(pieces):
    return pl.pallas_call(
        whole_kernel,
        out_shape=jax.ShapeDtypeStruct((RANK, TILES * LANES), F32),
        in_specs=[VMEM],
        out_specs=VMEM,
        compiler_params=pltpu.CompilerParams(vmem_limit_bytes=4 * 2**20),
        name="whole",
    )(pieces)


def body(n_col, flow, anchor, destination):
    pairs = [(i, i ^ 1) for i in range(n_col)]
    cores = [list(range(core, n_col, 2)) for core in range(2)]

    def over_row(x):
        return lax.all_to_all(x, "row", 0, 0, tiled=True)

    def over_chips(x):
        return lax.all_to_all(x, "col", 0, 0, axis_index_groups=cores, tiled=True)

    def to_other_core(x):
        return lax.ppermute(x, "col", pairs)

    anchor, destination = (anchor,), (destination,)
    for sweep in range(ITERS):
        first, last = sweep == 0, sweep == ITERS - 1
        mine, other, *rest = half("anchor", flow, anchor, destination, first=first)
        if first:
            (flow,) = rest
        new = update("col", over_chips(mine + to_other_core(other)), anchor)
        mine = over_chips(new)
        anchor = (mine, to_other_core(mine))
        sent, *rest = half("destination", flow, destination, anchor, emit_v=last)
        destination = (over_row(update("row", over_row(sent), destination)),)
    return rest[0], whole(destination[0])


def solution(mesh):
    in_specs = (P("row", "col"), P(None, "row"), P(None, "col"))
    out_specs = (P(None, "row"), P(None, "col"))
    return jax.shard_map(
        functools.partial(body, mesh.shape["col"]),
        mesh=mesh,
        in_specs=in_specs,
        out_specs=out_specs,
        check_vma=False,
    )
```

time: 148 us -> 137 us (0.926)
  blocking collectives: 122 us -> 96.3 us
  starting transfers between devices: 0 us -> 11.8 us
  waiting for transfers between devices: 0 us -> 4.11 us
  local copies, waits for them, and re-layouts: 1.92 us -> 0.01 us
    all_to_all x8, blocking collectives: 122 us -> 96.3 us  [the longest x4 48.4 us: over_row(): return lax.all_to_all(x, 'row', 0, 0, tiled=True)]
    ppermute x0 -> x4, starting transfers between devices: none -> 11.8 us  [to_other_core(): return lax.ppermute(x, 'col', pairs)]
    ppermute x0 -> x4, waiting for transfers between devices: none -> 4.11 us  [to_other_core(): return lax.ppermute(x, 'col', pairs)]
    unnamed x6 -> x4, local copies, waits for them, and re-layouts: 1.92 us -> 0.01 us
  transfers between devices with their start and end apart: 0 -> 4, of which waited for: 0 -> 4; matrix products, arithmetic and copies ran while one was open for 0% -> 0% of each run, Pallas kernels for 0% -> 0%
where the time goes in v3:
time: 137 us; the launch traced here: 136 us
  blocking collectives  96.3 us (70%)
  Pallas kernels  23 us (17%)
  starting transfers between devices  11.8 us (9%)
  waiting for transfers between devices  4.11 us (3%)
    all_to_all x4, blocking collectives, over_row(): return lax.all_to_all(x, 'row', 0, 0, tiled=True)  48.4 us
    all_to_all x4, blocking collectives, over_chips(): return lax.all_to_all(x, 'col', 0, 0, axis_index_groups=cores, tiled=True)  47.9 us
    pallas_call x4, Pallas kernels, half(): pl.pallas_call(functools.partial(half_kernel, kind, len(u), len(v), n_out...  21.6 us
    ppermute x4, starting transfers between devices, to_other_core(): return lax.ppermute(x, 'col', pairs)  11.8 us
    ppermute x4, waiting for transfers between devices, to_other_core(): return lax.ppermute(x, 'col', pairs)  4.11 us
  transfers between devices with their start and end apart: 4, of which 4 were waited for; matrix products, arithmetic and copies ran while one was open for 0% of the time, Pallas kernels for 0%

profile of v3, /device:TPU:1, one launch (start us, length us, event | category | flops | bytes accessed | tf_op | source)
XLA Modules:
  0.0 136.0 jit_solution(14358633915588907084)
XLA Ops:
  0.6 6.6 %half_anchor.2 = (f32[320,128]{1,0:T(8,128)S(1)}, f32[320,128]{1,0:T(8,128)S(1)}, f32[1536,1536]{1,0:T(8,128)S(1)}) custom-call(f32[1536,1536]{1,0:T(8,128)} %refs_0_.1, f32[48,1536]{1,0:T(8,128)} %old_ref.2, f32[48,1536]{1,0:T(8,128)} %old_ref.3), custom_call_target="tpu_custom_call" | custom-call | tf_op jit(solution)/shard_map/half_anchor/pallas_call | solution.py:177
  7.3 3.3 %collective-permute-start = (f32[320,128]{1,0:T(8,128)S(1)}, f32[320,128]{1,0:T(8,128)S(1)}, u32[]{:S(2)}, u32[]{:S(2)}) collective-permute-start(f32[320,128]{1,0:T(8,128)S(1)} %get-tuple-element.11), channel_id=1, source_target_pairs={{0,1},{1,0},{2,3},{3,2},{4,5},{5,4},{6,7},{7,6},{8,9},{9,8},{10,11... | collective-permute-start | bytes 491528 | tf_op jit(solution)/shard_map/ppermute | solution.py:261
  10.6 1.0 collective-permute-done
  11.6 14.9 %all_to_all.88 = f32[8,40,128]{2,1,0:T(8,128)S(1)} all-to-all(f32[8,40,128]{2,1,0:T(8,128)S(1)} %bitcast.36), channel_id=1, replica_groups={{0,2,4,6,8,10,12,14},{1,3,5,7,9,11,13,15},{16,18,20,22,24,26,28,30},{17..., dimensions={0} | all-to-all | bytes 327680 | tf_op jit(solution)/shard_map/all_to_all | solution.py:258
  26.6 0.1 update.4
  26.7 10.8 %all_to_all.89 = f32[8,40,128]{2,1,0:T(8,128)S(1)} all-to-all(f32[8,40,128]{2,1,0:T(8,128)S(1)} %bitcast.32), channel_id=1, replica_groups={{0,2,4,6,8,10,12,14},{1,3,5,7,9,11,13,15},{16,18,20,22,24,26,28,30},{17..., dimensions={0} | all-to-all | bytes 327680 | tf_op jit(solution)/shard_map/all_to_all | solution.py:258
  37.5 3.1 %collective-permute-start.1 = (f32[320,128]{1,0:T(8,128)S(1)}, f32[320,128]{1,0:T(8,128)S(1)}, u32[]{:S(2)}, u32[]{:S(2)}) collective-permute-start(f32[320,128]{1,0:T(8,128)S(1)} %bitcast.19), channel_id=1, source_target_pairs={{0,1},{1,0},{2,3},{3,2},{4,5},{5,4},{6,7},{7,6},{8,9},{9,8},{10,11... | collective-permute-start | bytes 491528 | tf_op jit(solution)/shard_map/ppermute | solution.py:261
  40.6 1.0 collective-permute-done.1.refs_3_.refs_2_
  41.6 5.0 %half_destination.2 = f32[640,128]{1,0:T(8,128)S(1)} custom-call(f32[1536,1536]{1,0:T(8,128)S(1)} %get-tuple-element.9.refs_0_, f32[48,1536]{1,0:T(8,128)S(1)} %copy-done, f32[320,128]{1,0:T(8,128)S(1)} %bitcast.20, f32[320,128]{1,0:T(8,128)S(1)} %collective-permute-done.1.refs_3_.refs_2_), custom_call_target="tpu_custom_call" | custom-call | tf_op jit(solution)/shard_map/half_destination/pallas_call | solution.py:177
  46.6 15.4 %all_to_all.90 = f32[16,40,128]{2,1,0:T(8,128)S(1)} all-to-all(f32[16,40,128]{2,1,0:T(8,128)S(1)} %bitcast.23), channel_id=1, replica_groups=mesh['row'=16,'col'=16] {'row'}, dimensions={0} | all-to-all | bytes 655360 | tf_op jit(solution)/shard_map/all_to_all | solution.py:255
  62.0 0.2 update.5
  62.2 10.8 %all_to_all.91 = f32[16,40,128]{2,1,0:T(8,128)S(1)} all-to-all(f32[16,40,128]{2,1,0:T(8,128)S(1)} %bitcast.28), channel_id=1, replica_groups=mesh['row'=16,'col'=16] {'row'}, dimensions={0} | all-to-all | bytes 655360 | tf_op jit(solution)/shard_map/all_to_all | solution.py:255
  72.9 5.0 %half_anchor.3 = (f32[320,128]{1,0:T(8,128)S(1)}, f32[320,128]{1,0:T(8,128)S(1)}) custom-call(f32[1536,1536]{1,0:T(8,128)S(1)} %get-tuple-element.9.refs_0_, f32[320,128]{1,0:T(8,128)S(1)} %bitcast.21, f32[320,128]{1,0:T(8,128)S(1)} %collective-permute-done.1.refs_3_.refs_2_, f32[640,128]{1,0:T(8,128)S(1)} %bitcast.16), custom_call_target="tpu_custom_call" | custom-call | tf_op jit(solution)/shard_map/half_anchor/pallas_call | solution.py:177
  77.9 2.7 %collective-permute-start.2 = (f32[320,128]{1,0:T(8,128)S(1)}, f32[320,128]{1,0:T(8,128)S(1)}, u32[]{:S(2)}, u32[]{:S(2)}) collective-permute-start(f32[320,128]{1,0:T(8,128)S(1)} %get-tuple-element.13), channel_id=1, source_target_pairs={{0,1},{1,0},{2,3},{3,2},{4,5},{5,4},{6,7},{7,6},{8,9},{9,8},{10,11... | collective-permute-start | bytes 491528 | tf_op jit(solution)/shard_map/ppermute | solution.py:261
  80.7 1.0 collective-permute-done.2
  81.7 11.5 %all_to_all.92 = f32[8,40,128]{2,1,0:T(8,128)S(1)} all-to-all(f32[8,40,128]{2,1,0:T(8,128)S(1)} %bitcast.37), channel_id=1, replica_groups={{0,2,4,6,8,10,12,14},{1,3,5,7,9,11,13,15},{16,18,20,22,24,26,28,30},{17..., dimensions={0} | all-to-all | bytes 327680 | tf_op jit(solution)/shard_map/all_to_all | solution.py:258
  93.4 10.8 %all_to_all.93 = f32[8,40,128]{2,1,0:T(8,128)S(1)} all-to-all(f32[8,40,128]{2,1,0:T(8,128)S(1)} %bitcast.30), channel_id=1, replica_groups={{0,2,4,6,8,10,12,14},{1,3,5,7,9,11,13,15},{16,18,20,22,24,26,28,30},{17..., dimensions={0} | all-to-all | bytes 327680 | tf_op jit(solution)/shard_map/all_to_all | solution.py:258
  104.1 2.7 %collective-permute-start.3 = (f32[320,128]{1,0:T(8,128)S(1)}, f32[320,128]{1,0:T(8,128)S(1)}, u32[]{:S(2)}, u32[]{:S(2)}) collective-permute-start(f32[320,128]{1,0:T(8,128)S(1)} %bitcast.33), channel_id=1, source_target_pairs={{0,1},{1,0},{2,3},{3,2},{4,5},{5,4},{6,7},{7,6},{8,9},{9,8},{10,11... | collective-permute-start | bytes 491528 | tf_op jit(solution)/shard_map/ppermute | solution.py:261
  106.8 1.0 collective-permute-done.3.refs_3_
  107.8 5.0 %half_destination.3 = (f32[640,128]{1,0:T(8,128)S(1)}, f32[48,1536]{1,0:T(8,128)}) custom-call(f32[1536,1536]{1,0:T(8,128)S(1)} %get-tuple-element.9.refs_0_, f32[640,128]{1,0:T(8,128)S(1)} %bitcast.17, f32[320,128]{1,0:T(8,128)S(1)} %bitcast.34, f32[320,128]{1,0:T(8,128)S(1)} %collective-permute-done.3.refs_3_), custom_call_target="tpu_custom_call" | custom-call | tf_op jit(solution)/shard_map/half_destination/pallas_call | solution.py:177
  112.8 11.5 %all_to_all.94 = f32[16,40,128]{2,1,0:T(8,128)S(1)} all-to-all(f32[16,40,128]{2,1,0:T(8,128)S(1)} %bitcast.35), channel_id=1, replica_groups=mesh['row'=16,'col'=16] {'row'}, dimensions={0} | all-to-all | bytes 655360 | tf_op jit(solution)/shard_map/all_to_all | solution.py:255
  124.3 0.2 update.7
  124.5 10.7 %all_to_all.95 = f32[16,40,128]{2,1,0:T(8,128)S(1)} all-to-all(f32[16,40,128]{2,1,0:T(8,128)S(1)} %bitcast.26), channel_id=1, replica_groups=mesh['row'=16,'col'=16] {'row'}, dimensions={0} | all-to-all | bytes 655360 | tf_op jit(solution)/shard_map/all_to_all | solution.py:255
  135.2 0.8 whole.1
  (7 shorter events, 0.2 us)
Async XLA Ops:
  0.6 41.0 %copy-start = (f32[48,1536]{1,0:T(8,128)S(1)}, f32[48,1536]{1,0:T(8,128)}, u32[]{:S(2)}) copy-start(f32[48,1536]{1,0:T(8,128)} %old_ref.3) | copy-start | bytes 884740
  0.6 25.9 %copy-start.1 = (f32[48,1536]{1,0:T(8,128)S(1)}, f32[48,1536]{1,0:T(8,128)}, u32[]{:S(2)}) copy-start(f32[48,1536]{1,0:T(8,128)} %old_ref.2) | copy-start | bytes 884740
  7.3 4.3 %collective-permute-start = (f32[320,128]{1,0:T(8,128)S(1)}, f32[320,128]{1,0:T(8,128)S(1)}, u32[]{:S(2)}, u32[]{:S(2)}) collective-permute-start(f32[320,128]{1,0:T(8,128)S(1)} %get-tuple-element.11), channel_id=1, source_target_pairs={{0,1},{1,0},{2,3},{3,2},{4,5},{5,4},{6,7},{7,6},{8,9},{9,8},{10,11... | collective-permute-start | bytes 491528 | tf_op jit(solution)/shard_map/ppermute | solution.py:261
  37.5 4.2 %collective-permute-start.1 = (f32[320,128]{1,0:T(8,128)S(1)}, f32[320,128]{1,0:T(8,128)S(1)}, u32[]{:S(2)}, u32[]{:S(2)}) collective-permute-start(f32[320,128]{1,0:T(8,128)S(1)} %bitcast.19), channel_id=1, source_target_pairs={{0,1},{1,0},{2,3},{3,2},{4,5},{5,4},{6,7},{7,6},{8,9},{9,8},{10,11... | collective-permute-start | bytes 491528 | tf_op jit(solution)/shard_map/ppermute | solution.py:261
  77.9 3.8 %collective-permute-start.2 = (f32[320,128]{1,0:T(8,128)S(1)}, f32[320,128]{1,0:T(8,128)S(1)}, u32[]{:S(2)}, u32[]{:S(2)}) collective-permute-start(f32[320,128]{1,0:T(8,128)S(1)} %get-tuple-element.13), channel_id=1, source_target_pairs={{0,1},{1,0},{2,3},{3,2},{4,5},{5,4},{6,7},{7,6},{8,9},{9,8},{10,11... | collective-permute-start | bytes 491528 | tf_op jit(solution)/shard_map/ppermute | solution.py:261
  104.1 3.7 %collective-permute-start.3 = (f32[320,128]{1,0:T(8,128)S(1)}, f32[320,128]{1,0:T(8,128)S(1)}, u32[]{:S(2)}, u32[]{:S(2)}) collective-permute-start(f32[320,128]{1,0:T(8,128)S(1)} %bitcast.33), channel_id=1, source_target_pairs={{0,1},{1,0},{2,3},{3,2},{4,5},{5,4},{6,7},{7,6},{8,9},{9,8},{10,11... | collective-permute-start | bytes 491528 | tf_op jit(solution)/shard_map/ppermute | solution.py:261

commit v4 on v3

--- a/solution.py
+++ b/solution.py
@@ -12,6 +12,7 @@
 LANES = 128
 COLS = 256
 ROWS = 256
+GROUP = 2
 
 F32 = jnp.float32
 BF16 = jnp.bfloat16
@@ -57,10 +58,13 @@
     (flow_in,), u_refs, v_refs, out_refs = take(1), take(n_u), take(n_v), take(n_out)
     (v_out,) = take(1) if emit_v else (None,)
     (flow,) = take(1) if first else (flow_in,)
-    v_f, v_t, v_cat, u_w, acc = take(5)
+    v_t, v_cat, u_w, acc = take(4)
     zones_u, zones_v = u_w.shape[1], v_t.shape[0]
     steps = zones_u // COLS
     core = lax.rem(lax.axis_index("col"), 2)
+    if emit_v:
+        v_buf, emit_sem = refs
+        emit = pltpu.make_async_copy(v_buf, v_out, emit_sem)
 
     def fetch(step):
         at = pl.ds(step * COLS, COLS)
@@ -75,55 +79,46 @@
         ]
         for copy in copies:
             copy.start()
-        fetch(0).start()
+        for step in range(GROUP):
+            fetch(step).start()
         for copy in copies:
             copy.wait()
-        fetch(1).start()
+        for step in range(GROUP, 2 * GROUP):
+            fetch(step).start()
         u_refs, v_refs = [u_buf], [v_buf]
 
-    sums = []
-    for part in range(PARTS):
-        total = None
-        low = part * PART
-        for tile in range(zones_u // LANES):
-            at = slice(tile * LANES, (tile + 1) * LANES)
-            high, low_term = split(load_tile(u_refs, core, part, tile))
-            for base in (0, 64):
-                u_w[base + low : base + low + PART, at] = high
-                u_w[128 + base + low : 128 + base + low + PART, at] = low_term
-        for tile in range(zones_v // LANES):
-            at = slice(tile * LANES, (tile + 1) * LANES)
+    gap = jnp.zeros((16, LANES), BF16)
+    for tile in range(zones_u // LANES):
+        at = slice(tile * LANES, (tile + 1) * LANES)
+        for part in range(PARTS):
+            low = part * PART
+            for base, term in zip((0, 128), split(load_tile(u_refs, core, part, tile))):
+                u_w[base + low : base + low + PART, at] = term
+                u_w[base + 64 + low : base + 64 + low + PART, at] = term
+        for base in (0, 64, 128, 192):
+            u_w[base + RANK : base + 64, at] = gap
+    sums = [None] * PARTS
+    gap = gap.astype(F32)
+    for tile in range(zones_v // LANES):
+        at = slice(tile * LANES, (tile + 1) * LANES)
+        heads, tails = [], []
+        for part in range(PARTS):
+            low = part * PART
             x = load_tile(v_refs, core, part, tile)
             high, low_term = split(x)
-            v_f[low : low + PART, at] = high.astype(F32)
-            v_f[64 + low : 64 + low + PART, at] = low_term.astype(F32)
             v_cat[low : low + PART, at] = high
             v_cat[RANK + low : RANK + low + PART, at] = low_term
-            total = x if total is None else total + x
+            heads.append(high.astype(F32))
+            tails.append(low_term.astype(F32))
+            sums[part] = x if tile == 0 else sums[part] + x
             if emit_v:
-                v_out[low : low + PART, at] = x
-        sums.append(total)
-    gap = jnp.zeros((16, zones_u), BF16)
-    for base in (0, 64, 128, 192):
-        u_w[base + RANK : base + 64, :] = gap
-    gap = jnp.zeros((16, zones_v), F32)
-    for base in (0, 64):
-        v_f[base + RANK : base + 64, :] = gap
-    for tile in range(zones_v // LANES):
-        at = slice(tile * LANES, (tile + 1) * LANES)
-        x = v_f[:, at].T.astype(BF16)
+                v_buf[low : low + PART, at] = x
+        x = jnp.concatenate([*heads, gap, *tails, gap], axis=0).T.astype(BF16)
         v_t[at, :LANES] = x
         v_t[at, LANES:] = x
 
-    def step_body(step, carry):
-        if first:
-            fetch(step).wait()
-
-            @pl.when(step + 2 < steps)
-            def _():
-                fetch(step + 2).start()
-
-        at = pl.ds(pl.multiple_of(step * COLS, COLS), COLS)
+    def slab(step):
+        at = slice(step * COLS, (step + 1) * COLS)
         weights = u_w[:, at]
         total = None
         for block in range(zones_v // ROWS):
@@ -138,9 +133,18 @@
             term += jnp.dot(left, tail, preferred_element_type=F32)
             total = term if total is None else total + term
         acc[:, at] = total[:RANK] + total[RANK:]
-        return carry
-
-    lax.fori_loop(0, steps, step_body, 0)
+
+    for step in range(steps):
+        if first and step % GROUP == 0:
+            for landed in range(step, step + GROUP):
+                fetch(landed).wait()
+            for later in range(step + 2 * GROUP, min(step + 3 * GROUP, steps)):
+                fetch(later).start()
+        slab(step)
+        if emit_v and step == 0:
+            emit.start()
+    if emit_v:
+        emit.wait()
 
     for part in range(PARTS):
         ranks = slice(part * PART, (part + 1) * PART)
@@ -155,18 +159,22 @@
     zones_u, zones_v = flow.shape if kind == "anchor" else flow.shape[::-1]
     n_out = 2 if kind == "anchor" else 1
     out_shape = [jax.ShapeDtypeStruct((PART // n_out * PIECE, LANES), F32)] * n_out
+    out_specs = [VMEM] * n_out
     if emit_v:
         out_shape.append(jax.ShapeDtypeStruct((RANK, zones_v), F32))
+        out_specs.append(pl.BlockSpec(memory_space=pl.ANY))
     scratch = [
-        pltpu.VMEM((LANES, zones_v), F32),
         pltpu.VMEM((zones_v, 2 * LANES), BF16),
         pltpu.VMEM((2 * RANK, zones_v), BF16),
         pltpu.VMEM((2 * LANES, zones_u), BF16),
         pltpu.VMEM((RANK, zones_u), F32),
     ]
     operands = [flow, *u, *v]
+    if emit_v:
+        scratch += [pltpu.VMEM((RANK, zones_v), F32), pltpu.SemaphoreType.DMA]
     if first:
         out_shape.append(pltpu.VMEM(flow.shape, F32))
+        out_specs.append(VMEM)
         operands = [pltpu.with_memory_space_constraint(x, pltpu.HBM) for x in operands]
         scratch += [
             pltpu.VMEM((RANK, zones_u), F32),
@@ -178,7 +186,7 @@
         functools.partial(half_kernel, kind, len(u), len(v), n_out, emit_v, first),
         out_shape=out_shape,
         in_specs=[pl.BlockSpec(memory_space=pl.ANY) if first else VMEM] * len(operands),
-        out_specs=[VMEM] * len(out_shape),
+        out_specs=out_specs,
         scratch_shapes=scratch,
         compiler_params=pltpu.CompilerParams(vmem_limit_bytes=30 * 2**20),
         name="half_" + kind,

time: 137 us -> 131 us (0.956)
  Pallas kernels: 23 us -> 17.5 us
    pallas_call x4, Pallas kernels: 21.6 us -> 16.1 us  [half(): pl.pallas_call(functools.partial(half_kernel, kind, len(u), len(v), n_out...]
where the time goes in v4:
time: 131 us
  blocking collectives  96.3 us (74%)
  Pallas kernels  17.5 us (13%)
  starting transfers between devices  12 us (9%)
  waiting for transfers between devices  4.11 us (3%)
    all_to_all x4, blocking collectives, over_row(): return lax.all_to_all(x, 'row', 0, 0, tiled=True)  48.4 us
    all_to_all x4, blocking collectives, over_chips(): return lax.all_to_all(x, 'col', 0, 0, axis_index_groups=cores, tiled=True)  47.9 us
    pallas_call x4, Pallas kernels, half(): pl.pallas_call(functools.partial(half_kernel, kind, len(u), len(v), n_out...  16.1 us
    ppermute x4, starting transfers between devices, to_other_core(): return lax.ppermute(x, 'col', pairs)  12 us
    ppermute x4, waiting for transfers between devices, to_other_core(): return lax.ppermute(x, 'col', pairs)  4.11 us
  transfers between devices with their start and end apart: 4, of which 4 were waited for; matrix products, arithmetic and copies ran while one was open for 0% of the time, Pallas kernels for 0%

profile of v4, /device:TPU:1, one launch (start us, length us, event | category | flops | bytes accessed | tf_op | source)
XLA Modules:
  0.0 130.6 jit_solution(5963543298608469780)
XLA Ops:
  0.6 6.1 %half_anchor.2 = (f32[320,128]{1,0:T(8,128)S(1)}, f32[320,128]{1,0:T(8,128)S(1)}, f32[1536,1536]{1,0:T(8,128)S(1)}) custom-call(f32[1536,1536]{1,0:T(8,128)} %refs_0_.1, f32[48,1536]{1,0:T(8,128)} %old_ref.2, f32[48,1536]{1,0:T(8,128)} %old_ref.3), custom_call_target="tpu_custom_call" | custom-call | tf_op jit(solution)/shard_map/half_anchor/pallas_call | solution.py:185
  6.8 3.3 %collective-permute-start = (f32[320,128]{1,0:T(8,128)S(1)}, f32[320,128]{1,0:T(8,128)S(1)}, u32[]{:S(2)}, u32[]{:S(2)}) collective-permute-start(f32[320,128]{1,0:T(8,128)S(1)} %get-tuple-element.11), channel_id=1, source_target_pairs={{0,1},{1,0},{2,3},{3,2},{4,5},{5,4},{6,7},{7,6},{8,9},{9,8},{10,11... | collective-permute-start | bytes 491528 | tf_op jit(solution)/shard_map/ppermute | solution.py:269
  10.1 1.0 collective-permute-done
  11.1 14.9 %all_to_all.88 = f32[8,40,128]{2,1,0:T(8,128)S(1)} all-to-all(f32[8,40,128]{2,1,0:T(8,128)S(1)} %bitcast.36), channel_id=1, replica_groups={{0,2,4,6,8,10,12,14},{1,3,5,7,9,11,13,15},{16,18,20,22,24,26,28,30},{17..., dimensions={0} | all-to-all | bytes 327680 | tf_op jit(solution)/shard_map/all_to_all | solution.py:266
  26.0 0.1 update.4
  26.2 10.8 %all_to_all.89 = f32[8,40,128]{2,1,0:T(8,128)S(1)} all-to-all(f32[8,40,128]{2,1,0:T(8,128)S(1)} %bitcast.32), channel_id=1, replica_groups={{0,2,4,6,8,10,12,14},{1,3,5,7,9,11,13,15},{16,18,20,22,24,26,28,30},{17..., dimensions={0} | all-to-all | bytes 327680 | tf_op jit(solution)/shard_map/all_to_all | solution.py:266
  37.0 3.1 %collective-permute-start.1 = (f32[320,128]{1,0:T(8,128)S(1)}, f32[320,128]{1,0:T(8,128)S(1)}, u32[]{:S(2)}, u32[]{:S(2)}) collective-permute-start(f32[320,128]{1,0:T(8,128)S(1)} %bitcast.19), channel_id=1, source_target_pairs={{0,1},{1,0},{2,3},{3,2},{4,5},{5,4},{6,7},{7,6},{8,9},{9,8},{10,11... | collective-permute-start | bytes 491528 | tf_op jit(solution)/shard_map/ppermute | solution.py:269
  40.1 1.0 collective-permute-done.1.refs_3_.refs_2_
  41.1 3.1 %half_destination.2 = f32[640,128]{1,0:T(8,128)S(1)} custom-call(f32[1536,1536]{1,0:T(8,128)S(1)} %get-tuple-element.9.refs_0_, f32[48,1536]{1,0:T(8,128)S(1)} %copy-done, f32[320,128]{1,0:T(8,128)S(1)} %bitcast.20, f32[320,128]{1,0:T(8,128)S(1)} %collective-permute-done.1.refs_3_.refs_2_), custom_call_target="tpu_custom_call" | custom-call | tf_op jit(solution)/shard_map/half_destination/pallas_call | solution.py:185
  44.2 15.4 %all_to_all.90 = f32[16,40,128]{2,1,0:T(8,128)S(1)} all-to-all(f32[16,40,128]{2,1,0:T(8,128)S(1)} %bitcast.23), channel_id=1, replica_groups=mesh['row'=16,'col'=16] {'row'}, dimensions={0} | all-to-all | bytes 655360 | tf_op jit(solution)/shard_map/all_to_all | solution.py:263
  59.6 0.2 update.5
  59.8 10.8 %all_to_all.91 = f32[16,40,128]{2,1,0:T(8,128)S(1)} all-to-all(f32[16,40,128]{2,1,0:T(8,128)S(1)} %bitcast.28), channel_id=1, replica_groups=mesh['row'=16,'col'=16] {'row'}, dimensions={0} | all-to-all | bytes 655360 | tf_op jit(solution)/shard_map/all_to_all | solution.py:263
  70.6 3.2 %half_anchor.3 = (f32[320,128]{1,0:T(8,128)S(1)}, f32[320,128]{1,0:T(8,128)S(1)}) custom-call(f32[1536,1536]{1,0:T(8,128)S(1)} %get-tuple-element.9.refs_0_, f32[320,128]{1,0:T(8,128)S(1)} %bitcast.21, f32[320,128]{1,0:T(8,128)S(1)} %collective-permute-done.1.refs_3_.refs_2_, f32[640,128]{1,0:T(8,128)S(1)} %bitcast.16), custom_call_target="tpu_custom_call" | custom-call | tf_op jit(solution)/shard_map/half_anchor/pallas_call | solution.py:185
  73.7 2.9 %collective-permute-start.2 = (f32[320,128]{1,0:T(8,128)S(1)}, f32[320,128]{1,0:T(8,128)S(1)}, u32[]{:S(2)}, u32[]{:S(2)}) collective-permute-start(f32[320,128]{1,0:T(8,128)S(1)} %get-tuple-element.13), channel_id=1, source_target_pairs={{0,1},{1,0},{2,3},{3,2},{4,5},{5,4},{6,7},{7,6},{8,9},{9,8},{10,11... | collective-permute-start | bytes 491528 | tf_op jit(solution)/shard_map/ppermute | solution.py:269
  76.6 1.0 collective-permute-done.2
  77.7 11.5 %all_to_all.92 = f32[8,40,128]{2,1,0:T(8,128)S(1)} all-to-all(f32[8,40,128]{2,1,0:T(8,128)S(1)} %bitcast.37), channel_id=1, replica_groups={{0,2,4,6,8,10,12,14},{1,3,5,7,9,11,13,15},{16,18,20,22,24,26,28,30},{17..., dimensions={0} | all-to-all | bytes 327680 | tf_op jit(solution)/shard_map/all_to_all | solution.py:266
  89.3 10.8 %all_to_all.93 = f32[8,40,128]{2,1,0:T(8,128)S(1)} all-to-all(f32[8,40,128]{2,1,0:T(8,128)S(1)} %bitcast.30), channel_id=1, replica_groups={{0,2,4,6,8,10,12,14},{1,3,5,7,9,11,13,15},{16,18,20,22,24,26,28,30},{17..., dimensions={0} | all-to-all | bytes 327680 | tf_op jit(solution)/shard_map/all_to_all | solution.py:266
  100.1 2.7 %collective-permute-start.3 = (f32[320,128]{1,0:T(8,128)S(1)}, f32[320,128]{1,0:T(8,128)S(1)}, u32[]{:S(2)}, u32[]{:S(2)}) collective-permute-start(f32[320,128]{1,0:T(8,128)S(1)} %bitcast.33), channel_id=1, source_target_pairs={{0,1},{1,0},{2,3},{3,2},{4,5},{5,4},{6,7},{7,6},{8,9},{9,8},{10,11... | collective-permute-start | bytes 491528 | tf_op jit(solution)/shard_map/ppermute | solution.py:269
  102.8 1.0 collective-permute-done.3.refs_3_
  103.8 3.7 %half_destination.3 = (f32[640,128]{1,0:T(8,128)S(1)}, f32[48,1536]{1,0:T(8,128)}) custom-call(f32[1536,1536]{1,0:T(8,128)S(1)} %get-tuple-element.9.refs_0_, f32[640,128]{1,0:T(8,128)S(1)} %bitcast.17, f32[320,128]{1,0:T(8,128)S(1)} %bitcast.34, f32[320,128]{1,0:T(8,128)S(1)} %collective-permute-done.3.refs_3_), custom_call_target="tpu_custom_call" | custom-call | tf_op jit(solution)/shard_map/half_destination/pallas_call | solution.py:185
  107.5 11.5 %all_to_all.94 = f32[16,40,128]{2,1,0:T(8,128)S(1)} all-to-all(f32[16,40,128]{2,1,0:T(8,128)S(1)} %bitcast.35), channel_id=1, replica_groups=mesh['row'=16,'col'=16] {'row'}, dimensions={0} | all-to-all | bytes 655360 | tf_op jit(solution)/shard_map/all_to_all | solution.py:263
  119.0 0.2 update.7
  119.1 10.7 %all_to_all.95 = f32[16,40,128]{2,1,0:T(8,128)S(1)} all-to-all(f32[16,40,128]{2,1,0:T(8,128)S(1)} %bitcast.26), channel_id=1, replica_groups=mesh['row'=16,'col'=16] {'row'}, dimensions={0} | all-to-all | bytes 655360 | tf_op jit(solution)/shard_map/all_to_all | solution.py:263
  129.9 0.8 whole.1
  (7 shorter events, 0.2 us)
Async XLA Ops:
  0.6 40.5 %copy-start = (f32[48,1536]{1,0:T(8,128)S(1)}, f32[48,1536]{1,0:T(8,128)}, u32[]{:S(2)}) copy-start(f32[48,1536]{1,0:T(8,128)} %old_ref.3) | copy-start | bytes 884740
  0.6 25.4 %copy-start.1 = (f32[48,1536]{1,0:T(8,128)S(1)}, f32[48,1536]{1,0:T(8,128)}, u32[]{:S(2)}) copy-start(f32[48,1536]{1,0:T(8,128)} %old_ref.2) | copy-start | bytes 884740
  6.8 4.3 %collective-permute-start = (f32[320,128]{1,0:T(8,128)S(1)}, f32[320,128]{1,0:T(8,128)S(1)}, u32[]{:S(2)}, u32[]{:S(2)}) collective-permute-start(f32[320,128]{1,0:T(8,128)S(1)} %get-tuple-element.11), channel_id=1, source_target_pairs={{0,1},{1,0},{2,3},{3,2},{4,5},{5,4},{6,7},{7,6},{8,9},{9,8},{10,11... | collective-permute-start | bytes 491528 | tf_op jit(solution)/shard_map/ppermute | solution.py:269
  37.0 4.2 %collective-permute-start.1 = (f32[320,128]{1,0:T(8,128)S(1)}, f32[320,128]{1,0:T(8,128)S(1)}, u32[]{:S(2)}, u32[]{:S(2)}) collective-permute-start(f32[320,128]{1,0:T(8,128)S(1)} %bitcast.19), channel_id=1, source_target_pairs={{0,1},{1,0},{2,3},{3,2},{4,5},{5,4},{6,7},{7,6},{8,9},{9,8},{10,11... | collective-permute-start | bytes 491528 | tf_op jit(solution)/shard_map/ppermute | solution.py:269
  73.7 3.9 %collective-permute-start.2 = (f32[320,128]{1,0:T(8,128)S(1)}, f32[320,128]{1,0:T(8,128)S(1)}, u32[]{:S(2)}, u32[]{:S(2)}) collective-permute-start(f32[320,128]{1,0:T(8,128)S(1)} %get-tuple-element.13), channel_id=1, source_target_pairs={{0,1},{1,0},{2,3},{3,2},{4,5},{5,4},{6,7},{7,6},{8,9},{9,8},{10,11... | collective-permute-start | bytes 491528 | tf_op jit(solution)/shard_map/ppermute | solution.py:269
  100.1 3.7 %collective-permute-start.3 = (f32[320,128]{1,0:T(8,128)S(1)}, f32[320,128]{1,0:T(8,128)S(1)}, u32[]{:S(2)}, u32[]{:S(2)}) collective-permute-start(f32[320,128]{1,0:T(8,128)S(1)} %bitcast.33), channel_id=1, source_target_pairs={{0,1},{1,0},{2,3},{3,2},{4,5},{5,4},{6,7},{7,6},{8,9},{9,8},{10,11... | collective-permute-start | bytes 491528 | tf_op jit(solution)/shard_map/ppermute | solution.py:269

commit v5 on v0

v5 whole, which is shorter than its diff:
```python
import functools

import jax
import jax.numpy as jnp
from jax import lax
from jax.experimental import pallas as pl
from jax.experimental.pallas import tpu as pltpu
from jax.sharding import PartitionSpec as P

ITERS = 2
RANK = 48
LANES = 128
COLS = 256
ROWS = 256
HALF = 768

F32 = jnp.float32
BF16 = jnp.bfloat16
VMEM = pl.BlockSpec(memory_space=pltpu.VMEM)
ANY = pl.BlockSpec(memory_space=pl.ANY)

PIECE = 40
ROW_FORM = (16, 3, 12)
HALF_FORM = (8, 6, 6)
PART = 16


def split(x):
    high = x.astype(BF16)
    return high, (x - high.astype(F32)).astype(BF16)


def lanes(tile):
    return slice(tile * LANES, (tile + 1) * LANES)


def load_tile(ref, part, tile, base=None):
    ranks = slice(part * PART, (part + 1) * PART)
    if ref.shape[0] == RANK:
        at = lanes(tile) if base is None else pl.ds(pl.multiple_of(base + tile * LANES, LANES), LANES)
        return ref[ranks, at]
    if ref.shape[0] == ROW_FORM[0] * PIECE:
        return ref[pl.ds(part * ROW_FORM[2] + tile, 16, stride=PIECE), :]
    rows = [(2 * part + i) * HALF_FORM[2] + tile for i in range(2)]
    return jnp.concatenate([ref[pl.ds(row, 8, stride=PIECE), :] for row in rows], axis=0)


def store_pieces(ref, total, sums):
    pieces, ranks, tiles = ROW_FORM if ref.shape[0] == ROW_FORM[0] * PIECE else HALF_FORM
    for rank in range(ranks):
        for tile in range(tiles):
            x = total[rank * pieces : (rank + 1) * pieces, lanes(tile)]
            ref[pl.ds(rank * tiles + tile, pieces, stride=PIECE), :] = x
    for part, x in enumerate(sums):
        if pieces == 8:
            x = x + pltpu.roll(x, LANES // 2, 1)
            left = lax.broadcasted_iota(jnp.int32, (8, LANES), 1) < LANES // 2
            x = jnp.where(left, x[:8], x[8:])
        ref[pl.ds(ranks * tiles + part, pieces, stride=PIECE), :] = x
    ref[pl.ds(PIECE - 1, pieces, stride=PIECE), :] = jnp.zeros((pieces, LANES), F32)


def put_moving(u_ref, u_w, base=None):
    gap = jnp.zeros((16, LANES), BF16)
    for tile in range(u_w.shape[1] // LANES):
        at = lanes(tile)
        for part in range(3):
            low = part * PART
            for first, term in zip((0, 128), split(load_tile(u_ref, part, tile, base))):
                u_w[first + low : first + low + PART, at] = term
                u_w[first + 64 + low : first + 64 + low + PART, at] = term
        for first in (0, 64, 128, 192):
            u_w[first + RANK : first + 64, at] = gap


def put_fixed(v_ref, v_t, v_cat):
    sums = [None] * 3
    gap = jnp.zeros((16, LANES), F32)
    for tile in range(v_t.shape[0] // LANES):
        at = lanes(tile)
        heads, tails = [], []
        for part in range(3):
            low = part * PART
            x = load_tile(v_ref, part, tile)
            high, low_term = split(x)
            v_cat[low : low + PART, at] = high
            v_cat[RANK + low : RANK + low + PART, at] = low_term
            heads.append(high.astype(F32))
            tails.append(low_term.astype(F32))
            sums[part] = x if tile == 0 else sums[part] + x
        x = jnp.concatenate([*heads, gap, *tails, gap], axis=0).T.astype(BF16)
        v_t[at, :LANES] = x
        v_t[at, LANES:] = x
    return sums


def slab(flow, turned, v_t, v_cat, u_w, step):
    at = slice(step * COLS, (step + 1) * COLS)
    weights = u_w[:, at]
    total = None
    for block in range(v_t.shape[0] // ROWS):
        rows = slice(block * ROWS, (block + 1) * ROWS)
        rebuilt = jnp.dot(v_t[rows, :], weights, preferred_element_type=F32)
        piece = flow[at, rows].T if turned else flow[rows, at]
        inverse = pl.reciprocal(rebuilt, approx=True)
        head = (piece * inverse).astype(BF16)
        tail = ((piece - rebuilt * head.astype(F32)) * inverse).astype(BF16)
        left = v_cat[:, rows]
        term = jnp.dot(left, head, preferred_element_type=F32)
        term += jnp.dot(left, tail, preferred_element_type=F32)
        total = term if total is None else total + term
    return total[:RANK] + total[RANK:]


def anchor_kernel(mine, first, load, flow_in, u_ref, v_ref, out_ref, *refs):
    refs = list(refs)
    flow = refs.pop(0) if first else flow_in
    v_t, v_cat, u_w, acc = refs[:4]
    core = lax.rem(lax.axis_index("col"), 2)
    base = pl.multiple_of((core if mine else 1 - core) * HALF, HALF)
    steps = HALF // COLS
    if first:
        sem = refs[4]

        def fetch(step):
            there = pl.ds(pl.multiple_of(base + step * COLS, COLS), COLS)
            return pltpu.make_async_copy(
                flow_in.at[there, :], flow.at[step * COLS : (step + 1) * COLS, :], sem.at[step]
            )

        if load:
            u_buf, v_buf, factor_sem = refs[5:]
            copies = [
                pltpu.make_async_copy(u_ref, u_buf, factor_sem.at[0]),
                pltpu.make_async_copy(v_ref, v_buf, factor_sem.at[1]),
            ]
            for copy in copies:
                copy.start()
            u_ref, v_ref = u_buf, v_buf
        fetch(0).start()
        fetch(1).start()
        if load:
            for copy in copies:
                copy.wait()
        fetch(2).start()
    put_moving(u_ref, u_w, base if u_ref.shape[0] == RANK else None)
    sums = put_fixed(v_ref, v_t, v_cat)
    for step in range(steps):
        if first:
            fetch(step).wait()
        acc[:, step * COLS : (step + 1) * COLS] = slab(flow, True, v_t, v_cat, u_w, step)
    store_pieces(out_ref, acc, sums)


def cost(zones_u, zones_v):
    work = zones_u * zones_v
    return pl.CostEstimate(flops=1000 * work, bytes_accessed=4 * work, transcendentals=work)


def factor_scratch(zones_u, zones_v):
    return [
        pltpu.VMEM((zones_v, 2 * LANES), BF16),
        pltpu.VMEM((2 * RANK, zones_v), BF16),
        pltpu.VMEM((2 * LANES, zones_u), BF16),
        pltpu.VMEM((RANK, zones_u), F32),
    ]


def anchor_half(mine, flow, u, v, first=False):
    zones = flow.shape[1]
    load = first and not mine
    out_shape = [jax.ShapeDtypeStruct((HALF_FORM[0] * PIECE, LANES), F32)]
    scratch = factor_scratch(HALF, zones)
    in_specs = [VMEM] * 3
    if first:
        out_shape.append(pltpu.VMEM((HALF, zones), F32))
        scratch.append(pltpu.SemaphoreType.DMA((HALF // COLS,)))
        in_specs[0] = ANY
        flow = pltpu.with_memory_space_constraint(flow, pltpu.HBM)
    if load:
        in_specs = [ANY] * 3
        u, v = (pltpu.with_memory_space_constraint(x, pltpu.HBM) for x in (u, v))
        scratch += [pltpu.VMEM(u.shape, F32), pltpu.VMEM(v.shape, F32), pltpu.SemaphoreType.DMA((2,))]
    return pl.pallas_call(
        functools.partial(anchor_kernel, mine, first, load),
        out_shape=out_shape,
        in_specs=in_specs,
        out_specs=[VMEM] * len(out_shape),
        scratch_shapes=scratch,
        cost_estimate=cost(HALF, zones),
        compiler_params=pltpu.CompilerParams(vmem_limit_bytes=24 * 2**20),
        name="anchor_mine" if mine else "anchor_other",
    )(flow, u, v)


def near_kernel(flow, u_ref, v_ref, out_ref, v_t, v_cat, u_w):
    put_moving(u_ref, u_w)
    put_fixed(v_ref, v_t, v_cat)
    for step in range(u_w.shape[1] // COLS):
        out_ref[:, step * COLS : (step + 1) * COLS] = slab(flow, False, v_t, v_cat, u_w, step)


def far_kernel(emit, flow, u_ref, v_ref, near_ref, mine_ref, out_ref, *refs):
    refs = list(refs)
    v_out = refs.pop(0) if emit else None
    v_t, v_cat, u_w, acc = refs
    core = lax.rem(lax.axis_index("col"), 2)
    sums = put_fixed(v_ref, v_t, v_cat)
    for tile in range(HALF_FORM[2]):
        for part in range(3):
            x = load_tile(mine_ref, part, tile)
            sums[part] = sums[part] + x
            if emit:
                for y, owner in ((x, core), (load_tile(v_ref, part, tile), 1 - core)):
                    at = pl.ds(pl.multiple_of(owner * HALF + tile * LANES, LANES), LANES)
                    v_out[part * PART : (part + 1) * PART, at] = y
    put_moving(u_ref, u_w)
    for step in range(u_w.shape[1] // COLS):
        at = slice(step * COLS, (step + 1) * COLS)
        acc[:, at] = near_ref[:, at] + slab(flow, False, v_t, v_cat, u_w, step)
    store_pieces(out_ref, acc, sums)


def destination_half(flow_mine, flow_other, u, mine, other, emit):
    zones = flow_mine.shape[1]
    params = dict(
        cost_estimate=cost(zones, HALF),
        compiler_params=pltpu.CompilerParams(vmem_limit_bytes=24 * 2**20),
    )
    near = pl.pallas_call(
        near_kernel,
        out_shape=jax.ShapeDtypeStruct((RANK, zones), F32),
        in_specs=[VMEM] * 3,
        out_specs=VMEM,
        scratch_shapes=factor_scratch(zones, HALF)[:3],
        name="destination_near",
        **params,
    )(flow_mine, u, mine)
    out_shape = [jax.ShapeDtypeStruct((ROW_FORM[0] * PIECE, LANES), F32)]
    if emit:
        out_shape.append(jax.ShapeDtypeStruct((RANK, 2 * HALF), F32))
    return pl.pallas_call(
        functools.partial(far_kernel, emit),
        out_shape=out_shape,
        in_specs=[VMEM] * 5,
        out_specs=[VMEM] * len(out_shape),
        scratch_shapes=factor_scratch(zones, HALF),
        name="destination_far",
        **params,
    )(flow_other, u, other, near, mine)


def update_kernel(axis, got_ref, old_ref, out_ref, old):
    me = lax.axis_index(axis)
    pieces, ranks, tiles = ROW_FORM if axis == "row" else HALF_FORM
    if axis == "col":
        me, core = me // 2, lax.rem(me, 2)
    if old_ref.shape[0] == RANK:
        zones = slice(None) if axis == "row" else pl.ds(pl.multiple_of(core * HALF, HALF), HALF)
        for rank in range(ranks):
            x = old_ref[rank * pieces : (rank + 1) * pieces, zones]
            here = lax.broadcasted_iota(jnp.int32, x.shape, 0) == me
            x = jnp.sum(jnp.where(here, x, 0.0), axis=0, keepdims=True)
            for tile in range(tiles):
                row = rank * tiles + tile
                old[row : row + 1, :] = x[:, lanes(tile)]
        old[ranks * tiles :, :] = jnp.zeros((PIECE - ranks * tiles, LANES), F32)
        before = old[...]
    else:
        before = old_ref[pl.ds(pl.multiple_of(me * PIECE, 8), PIECE), :]
    total = got_ref[:PIECE, :]
    for peer in range(1, pieces):
        total = total + got_ref[peer * PIECE : (peer + 1) * PIECE, :]
    row = lax.broadcasted_iota(jnp.int32, (PIECE, LANES), 0)
    norm = jnp.zeros((PIECE, LANES), F32)
    for rank in range(ranks):
        at = ranks * tiles + (rank if axis == "row" else rank // 2)
        x = total[at : at + 1, :]
        if axis == "col":
            left = lax.broadcasted_iota(jnp.int32, x.shape, 1) < LANES // 2
            x = jnp.where(left, x, 0.0) if rank % 2 == 0 else jnp.where(left, 0.0, x)
        norm = jnp.where(row >= rank * tiles, jnp.sum(x), norm)
    new = jnp.where(row < ranks * tiles, before * total / norm, 0.0)
    for peer in range(pieces):
        out_ref[peer * PIECE : (peer + 1) * PIECE, :] = new


def update(axis, got, old):
    return pl.pallas_call(
        functools.partial(update_kernel, axis),
        out_shape=jax.ShapeDtypeStruct(got.shape, F32),
        in_specs=[VMEM, VMEM],
        out_specs=VMEM,
        scratch_shapes=[pltpu.VMEM((PIECE, LANES), F32)],
        compiler_params=pltpu.CompilerParams(vmem_limit_bytes=4 * 2**20),
        name="update",
    )(got, old)


def whole_kernel(in_ref, out_ref):
    for part in range(3):
        for tile in range(ROW_FORM[2]):
            out_ref[part * PART : (part + 1) * PART, lanes(tile)] = load_tile(in_ref, part, tile)


def whole(pieces):
    return pl.pallas_call(
        whole_kernel,
        out_shape=jax.ShapeDtypeStruct((RANK, ROW_FORM[2] * LANES), F32),
        in_specs=[VMEM],
        out_specs=VMEM,
        compiler_params=pltpu.CompilerParams(vmem_limit_bytes=4 * 2**20),
        name="whole",
    )(pieces)


def body(n_col, flow, anchor, destination):
    pairs = [(i, i ^ 1) for i in range(n_col)]
    cores = [list(range(core, n_col, 2)) for core in range(2)]

    def over_row(x):
        return lax.all_to_all(x, "row", 0, 0, tiled=True)

    def over_chips(x):
        return lax.all_to_all(x, "col", 0, 0, axis_index_groups=cores, tiled=True)

    def to_other(x):
        return lax.ppermute(x, "col", pairs)

    mine, other, flow_mine, flow_other = anchor, anchor, flow, flow
    for sweep in range(ITERS):
        first, last = sweep == 0, sweep == ITERS - 1
        sent, *rest = anchor_half(False, flow_other, other, destination, first)
        flow_other = rest[0] if first else flow_other
        got = to_other(sent)
        sent, *rest = anchor_half(True, flow_mine, mine, destination, first)
        flow_mine = rest[0] if first else flow_mine
        mine = over_chips(update("col", over_chips(sent + got), mine))
        other = to_other(mine)
        sent, *rest = destination_half(flow_mine, flow_other, destination, mine, other, last)
        destination = over_row(update("row", over_row(sent), destination))
    return rest[0], whole(destination)


def solution(mesh):
    in_specs = (P("row", "col"), P(None, "row"), P(None, "col"))
    out_specs = (P(None, "row"), P(None, "col"))
    return jax.shard_map(
        functools.partial(body, mesh.shape["col"]),
        mesh=mesh,
        in_specs=in_specs,
        out_specs=out_specs,
        check_vma=False,
    )
```

time: 505 us -> 131 us (0.26); the launches traced: 495 us -> 131 us
  waiting for transfers between devices: 282 us -> 0.05 us
  matrix products: 73.4 us -> 0 us
  Pallas kernels: 0 us -> 20.2 us
  blocking collectives: 120 us -> 99.9 us
  between operations: 14.3 us -> 0.77 us
  starting transfers between devices: 0.16 us -> 9.97 us
  other arithmetic: 5.38 us -> 0.04 us
    psum x4 -> x0, waiting for transfers between devices: 282 us -> none  [the longest x2 164 us: scale_anchor(): numerator, totals = lax.psum((partial_value, local_totals), 'col')]
    psum x4 -> x0, blocking collectives: 120 us -> none  [the longest x2 66.4 us: scale_destination(): numerator, totals = lax.psum((partial_value, local_totals), 'row')]
    all_to_all x0 -> x8, blocking collectives: none -> 99.9 us  [the longest x4 50.2 us: over_chips(): return lax.all_to_all(x, 'col', 0, 0, axis_index_groups=cores, tiled=True)]
    dot_general x8 -> x0, matrix products: 73.4 us -> none  [contract(): lax.dot_general(left, right, (dims, ((), ())), precision=HIGH, preferred_...]
    pallas_call x0 -> x13, Pallas kernels: none -> 20.2 us  [the longest x4 11.5 us: anchor_half(): pl.pallas_call(functools.partial(anchor_kernel, mine, first, load), out_s...]
    ppermute x0 -> x4, starting transfers between devices: none -> 9.97 us  [to_other(): return lax.ppermute(x, 'col', pairs)]
  transfers between devices with their start and end apart: 4 -> 4, of which waited for: 4 -> 0; matrix products, arithmetic and copies ran while one was open for 0% -> 0% of each run, Pallas kernels for 0% -> 7%
where the time goes in v5:
time: 131 us
  blocking collectives  99.9 us (76%)
  Pallas kernels  20.2 us (15%)
  starting transfers between devices  9.97 us (8%)
    all_to_all x4, blocking collectives, over_chips(): return lax.all_to_all(x, 'col', 0, 0, axis_index_groups=cores, tiled=True)  50.2 us
    all_to_all x4, blocking collectives, over_row(): return lax.all_to_all(x, 'row', 0, 0, tiled=True)  49.7 us
    pallas_call x4, Pallas kernels, anchor_half(): pl.pallas_call(functools.partial(anchor_kernel, mine, first, load), out_s...  11.5 us
    ppermute x4, starting transfers between devices, to_other(): return lax.ppermute(x, 'col', pairs)  9.97 us
    pallas_call x2, Pallas kernels, destination_half(): pl.pallas_call(functools.partial(far_kernel, emit), out_shape=out_shape,...  3.98 us
    pallas_call x2, Pallas kernels, destination_half(): pl.pallas_call(near_kernel, out_shape=jax.ShapeDtypeStruct((RANK, zones),...  3.34 us
  transfers between devices with their start and end apart: 4, of which 0 were waited for; matrix products, arithmetic and copies ran while one was open for 0% of the time, Pallas kernels for 7%

profile of v5, /device:TPU:1, one launch (start us, length us, event | category | flops | bytes accessed | tf_op | source)
XLA Modules:
  0.0 130.9 jit_solution(5160250764766551314)
XLA Ops:
  0.6 4.0 %anchor_other.2 = (f32[320,128]{1,0:T(8,128)S(1)}, f32[768,1536]{1,0:T(8,128)S(1)}) custom-call(f32[1536,1536]{1,0:T(8,128)} %flow_in.3, f32[48,1536]{1,0:T(8,128)} %old_ref.2, f32[48,1536]{1,0:T(8,128)} %old_ref.3), custom_call_target="tpu_custom_call" | custom-call | flops 1179648000 | bytes 4718592 | tf_op jit(solution)/shard_map/anchor_other/pallas_call | solution.py:184
  4.7 3.3 %collective-permute-start = (f32[320,128]{1,0:T(8,128)S(1)}, f32[320,128]{1,0:T(8,128)S(1)}, u32[]{:S(2)}, u32[]{:S(2)}) collective-permute-start(f32[320,128]{1,0:T(8,128)S(1)} %get-tuple-element.10), channel_id=1, source_target_pairs={{0,1},{1,0},{2,3},{3,2},{4,5},{5,4},{6,7},{7,6},{8,9},{9,8},{10,11... | collective-permute-start | bytes 491528 | tf_op jit(solution)/shard_map/ppermute | solution.py:328
  7.9 3.8 %anchor_mine.2 = (f32[320,128]{1,0:T(8,128)S(1)}, f32[768,1536]{1,0:T(8,128)S(1)}) custom-call(f32[1536,1536]{1,0:T(8,128)} %flow_in.3, f32[48,1536]{1,0:T(8,128)S(1)} %copy-done.1, f32[48,1536]{1,0:T(8,128)S(1)} %copy-done), custom_call_target="tpu_custom_call" | custom-call | flops 1179648000 | bytes 4718592 | tf_op jit(solution)/shard_map/anchor_mine/pallas_call | solution.py:184
  11.8 15.5 %all_to_all.88 = f32[8,40,128]{2,1,0:T(8,128)S(1)} all-to-all(f32[8,40,128]{2,1,0:T(8,128)S(1)} %bitcast.40), channel_id=1, replica_groups={{0,2,4,6,8,10,12,14},{1,3,5,7,9,11,13,15},{16,18,20,22,24,26,28,30},{17..., dimensions={0} | all-to-all | bytes 327680 | tf_op jit(solution)/shard_map/all_to_all | solution.py:325
  27.3 0.1 update.4
  27.4 10.8 %all_to_all.89 = f32[8,40,128]{2,1,0:T(8,128)S(1)} all-to-all(f32[8,40,128]{2,1,0:T(8,128)S(1)} %bitcast.38), channel_id=1, replica_groups={{0,2,4,6,8,10,12,14},{1,3,5,7,9,11,13,15},{16,18,20,22,24,26,28,30},{17..., dimensions={0} | all-to-all | bytes 327680 | tf_op jit(solution)/shard_map/all_to_all | solution.py:325
  38.2 2.6 %collective-permute-start.1 = (f32[320,128]{1,0:T(8,128)S(1)}, f32[320,128]{1,0:T(8,128)S(1)}, u32[]{:S(2)}, u32[]{:S(2)}) collective-permute-start(f32[320,128]{1,0:T(8,128)S(1)} %bitcast.21), channel_id=1, source_target_pairs={{0,1},{1,0},{2,3},{3,2},{4,5},{5,4},{6,7},{7,6},{8,9},{9,8},{10,11... | collective-permute-start | bytes 491528 | tf_op jit(solution)/shard_map/ppermute | solution.py:328
  40.8 1.7 %destination_near.2.near_ref = f32[48,1536]{1,0:T(8,128)S(1)} custom-call(f32[768,1536]{1,0:T(8,128)S(1)} %get-tuple-element.11.flow.flow_in, f32[48,1536]{1,0:T(8,128)S(1)} %copy-done, f32[320,128]{1,0:T(8,128)S(1)} %bitcast.22), custom_call_target="tpu_custom_call" | custom-call | flops 1179648000 | bytes 4718592 | tf_op jit(solution)/shard_map/destination_near/pallas_call | solution.py:230
  42.5 1.7 %destination_far.2 = f32[640,128]{1,0:T(8,128)S(1)} custom-call(f32[768,1536]{1,0:T(8,128)S(1)} %get-tuple-element.8.flow.flow_in, f32[48,1536]{1,0:T(8,128)S(1)} %copy-done, f32[320,128]{1,0:T(8,128)S(1)} %collective-permute-done.1.v_ref.u_ref, f32[48,1536]{1,0:T(8,128)S(1)} %destination_near.2.near_ref, f32[320,128]{1,0:T(8,128)S(1)} %bitcast.23), custom_call_target="tpu_custom_call" | custom-call | flops 1179648000 | bytes 4718592 | tf_op jit(solution)/shard_map/destination_far/pallas_call | solution.py:242
  44.2 15.6 %all_to_all.90 = f32[16,40,128]{2,1,0:T(8,128)S(1)} all-to-all(f32[16,40,128]{2,1,0:T(8,128)S(1)} %bitcast.29), channel_id=1, replica_groups=mesh['row'=16,'col'=16] {'row'}, dimensions={0} | all-to-all | bytes 655360 | tf_op jit(solution)/shard_map/all_to_all | solution.py:322
  59.8 0.2 update.5
  59.9 11.3 %all_to_all.91 = f32[16,40,128]{2,1,0:T(8,128)S(1)} all-to-all(f32[16,40,128]{2,1,0:T(8,128)S(1)} %bitcast.34), channel_id=1, replica_groups=mesh['row'=16,'col'=16] {'row'}, dimensions={0} | all-to-all | bytes 655360 | tf_op jit(solution)/shard_map/all_to_all | solution.py:322
  71.2 1.8 %anchor_other.3 = f32[320,128]{1,0:T(8,128)S(1)} custom-call(f32[768,1536]{1,0:T(8,128)S(1)} %get-tuple-element.8.flow.flow_in, f32[320,128]{1,0:T(8,128)S(1)} %collective-permute-done.1.v_ref.u_ref, f32[640,128]{1,0:T(8,128)S(1)} %bitcast.16), custom_call_target="tpu_custom_call" | custom-call | flops 1179648000 | bytes 4718592 | tf_op jit(solution)/shard_map/anchor_other/pallas_call | solution.py:184
  73.0 2.3 %collective-permute-start.2 = (f32[320,128]{1,0:T(8,128)S(1)}, f32[320,128]{1,0:T(8,128)S(1)}, u32[]{:S(2)}, u32[]{:S(2)}) collective-permute-start(f32[320,128]{1,0:T(8,128)S(1)} %anchor_other.3), channel_id=1, source_target_pairs={{0,1},{1,0},{2,3},{3,2},{4,5},{5,4},{6,7},{7,6},{8,9},{9,8},{10,11... | collective-permute-start | bytes 491528 | tf_op jit(solution)/shard_map/ppermute | solution.py:328
  75.3 1.8 %anchor_mine.3 = f32[320,128]{1,0:T(8,128)S(1)} custom-call(f32[768,1536]{1,0:T(8,128)S(1)} %get-tuple-element.11.flow.flow_in, f32[320,128]{1,0:T(8,128)S(1)} %bitcast.24, f32[640,128]{1,0:T(8,128)S(1)} %bitcast.17), custom_call_target="tpu_custom_call" | custom-call | flops 1179648000 | bytes 4718592 | tf_op jit(solution)/shard_map/anchor_mine/pallas_call | solution.py:184
  77.2 12.7 %all_to_all.92 = f32[8,40,128]{2,1,0:T(8,128)S(1)} all-to-all(f32[8,40,128]{2,1,0:T(8,128)S(1)} %bitcast.41), channel_id=1, replica_groups={{0,2,4,6,8,10,12,14},{1,3,5,7,9,11,13,15},{16,18,20,22,24,26,28,30},{17..., dimensions={0} | all-to-all | bytes 327680 | tf_op jit(solution)/shard_map/all_to_all | solution.py:325
  90.0 11.4 %all_to_all.93 = f32[8,40,128]{2,1,0:T(8,128)S(1)} all-to-all(f32[8,40,128]{2,1,0:T(8,128)S(1)} %bitcast.36), channel_id=1, replica_groups={{0,2,4,6,8,10,12,14},{1,3,5,7,9,11,13,15},{16,18,20,22,24,26,28,30},{17..., dimensions={0} | all-to-all | bytes 327680 | tf_op jit(solution)/shard_map/all_to_all | solution.py:325
  101.4 1.8 %collective-permute-start.3 = (f32[320,128]{1,0:T(8,128)S(1)}, f32[320,128]{1,0:T(8,128)S(1)}, u32[]{:S(2)}, u32[]{:S(2)}) collective-permute-start(f32[320,128]{1,0:T(8,128)S(1)} %bitcast.26), channel_id=1, source_target_pairs={{0,1},{1,0},{2,3},{3,2},{4,5},{5,4},{6,7},{7,6},{8,9},{9,8},{10,11... | collective-permute-start | bytes 491528 | tf_op jit(solution)/shard_map/ppermute | solution.py:328
  103.1 1.7 %destination_near.3.near_ref = f32[48,1536]{1,0:T(8,128)S(1)} custom-call(f32[768,1536]{1,0:T(8,128)S(1)} %get-tuple-element.11.flow.flow_in, f32[640,128]{1,0:T(8,128)S(1)} %bitcast.18, f32[320,128]{1,0:T(8,128)S(1)} %bitcast.27), custom_call_target="tpu_custom_call" | custom-call | flops 1179648000 | bytes 4718592 | tf_op jit(solution)/shard_map/destination_near/pallas_call | solution.py:230
  104.8 2.3 %destination_far.3 = (f32[640,128]{1,0:T(8,128)S(1)}, f32[48,1536]{1,0:T(8,128)}) custom-call(f32[768,1536]{1,0:T(8,128)S(1)} %get-tuple-element.8.flow.flow_in, f32[640,128]{1,0:T(8,128)S(1)} %bitcast.19, f32[320,128]{1,0:T(8,128)S(1)} %collective-permute-done.3.v_ref, f32[48,1536]{1,0:T(8,128)S(1)} %destination_near.3.near_ref, f32[320,128]{1,0:T(8,128)S(1)} %bitcast.28), custom_call_target="tpu_custom_call" | custom-call | flops 1179648000 | bytes 4718592 | tf_op jit(solution)/shard_map/destination_far/pallas_call | solution.py:242
  107.1 11.6 %all_to_all.94 = f32[16,40,128]{2,1,0:T(8,128)S(1)} all-to-all(f32[16,40,128]{2,1,0:T(8,128)S(1)} %bitcast.39), channel_id=1, replica_groups=mesh['row'=16,'col'=16] {'row'}, dimensions={0} | all-to-all | bytes 655360 | tf_op jit(solution)/shard_map/all_to_all | solution.py:322
  118.7 0.2 update.7
  118.9 11.3 %all_to_all.95 = f32[16,40,128]{2,1,0:T(8,128)S(1)} all-to-all(f32[16,40,128]{2,1,0:T(8,128)S(1)} %bitcast.32), channel_id=1, replica_groups=mesh['row'=16,'col'=16] {'row'}, dimensions={0} | all-to-all | bytes 655360 | tf_op jit(solution)/shard_map/all_to_all | solution.py:322
  130.1 0.8 whole.1
  (11 shorter events, 0.2 us)
Async XLA Ops:
  0.6 7.3 %copy-start = (f32[48,1536]{1,0:T(8,128)S(1)}, f32[48,1536]{1,0:T(8,128)}, u32[]{:S(2)}) copy-start(f32[48,1536]{1,0:T(8,128)} %old_ref.3) | copy-start | bytes 884740
  0.6 7.3 %copy-start.1 = (f32[48,1536]{1,0:T(8,128)S(1)}, f32[48,1536]{1,0:T(8,128)}, u32[]{:S(2)}) copy-start(f32[48,1536]{1,0:T(8,128)} %old_ref.2) | copy-start | bytes 884740
  4.7 7.1 %collective-permute-start = (f32[320,128]{1,0:T(8,128)S(1)}, f32[320,128]{1,0:T(8,128)S(1)}, u32[]{:S(2)}, u32[]{:S(2)}) collective-permute-start(f32[320,128]{1,0:T(8,128)S(1)} %get-tuple-element.10), channel_id=1, source_target_pairs={{0,1},{1,0},{2,3},{3,2},{4,5},{5,4},{6,7},{7,6},{8,9},{9,8},{10,11... | collective-permute-start | bytes 491528 | tf_op jit(solution)/shard_map/ppermute | solution.py:328
  38.2 4.3 %collective-permute-start.1 = (f32[320,128]{1,0:T(8,128)S(1)}, f32[320,128]{1,0:T(8,128)S(1)}, u32[]{:S(2)}, u32[]{:S(2)}) collective-permute-start(f32[320,128]{1,0:T(8,128)S(1)} %bitcast.21), channel_id=1, source_target_pairs={{0,1},{1,0},{2,3},{3,2},{4,5},{5,4},{6,7},{7,6},{8,9},{9,8},{10,11... | collective-permute-start | bytes 491528 | tf_op jit(solution)/shard_map/ppermute | solution.py:328
  73.0 4.2 %collective-permute-start.2 = (f32[320,128]{1,0:T(8,128)S(1)}, f32[320,128]{1,0:T(8,128)S(1)}, u32[]{:S(2)}, u32[]{:S(2)}) collective-permute-start(f32[320,128]{1,0:T(8,128)S(1)} %anchor_other.3), channel_id=1, source_target_pairs={{0,1},{1,0},{2,3},{3,2},{4,5},{5,4},{6,7},{7,6},{8,9},{9,8},{10,11... | collective-permute-start | bytes 491528 | tf_op jit(solution)/shard_map/ppermute | solution.py:328
  101.4 3.5 %collective-permute-start.3 = (f32[320,128]{1,0:T(8,128)S(1)}, f32[320,128]{1,0:T(8,128)S(1)}, u32[]{:S(2)}, u32[]{:S(2)}) collective-permute-start(f32[320,128]{1,0:T(8,128)S(1)} %bitcast.26), channel_id=1, source_target_pairs={{0,1},{1,0},{2,3},{3,2},{4,5},{5,4},{6,7},{7,6},{8,9},{9,8},{10,11... | collective-permute-start | bytes 491528 | tf_op jit(solution)/shard_map/ppermute | solution.py:328

commit v6 on v5

--- a/solution.py
+++ b/solution.py
@@ -112,44 +112,46 @@
     return total[:RANK] + total[RANK:]
 
 
-def anchor_kernel(mine, first, load, flow_in, u_ref, v_ref, out_ref, *refs):
+def anchor_kernel(mine, first, flow_in, u_ref, v_ref, out_ref, *refs):
     refs = list(refs)
-    flow = refs.pop(0) if first else flow_in
+    flow, flow_next = (refs.pop(0), refs.pop(0)) if first else (flow_in, None)
     v_t, v_cat, u_w, acc = refs[:4]
     core = lax.rem(lax.axis_index("col"), 2)
-    base = pl.multiple_of((core if mine else 1 - core) * HALF, HALF)
+    owner = core if mine else 1 - core
+    base = pl.multiple_of(owner * HALF, HALF)
     steps = HALF // COLS
+
+    def fetch(step):
+        half, into = (owner, flow) if step < steps else (1 - owner, flow_next)
+        low = step % steps * COLS
+        there = pl.ds(pl.multiple_of(half * HALF + low, COLS), COLS)
+        return pltpu.make_async_copy(flow_in.at[there, :], into.at[low : low + COLS, :], sem.at[step])
+
     if first:
-        sem = refs[4]
-
-        def fetch(step):
-            there = pl.ds(pl.multiple_of(base + step * COLS, COLS), COLS)
-            return pltpu.make_async_copy(
-                flow_in.at[there, :], flow.at[step * COLS : (step + 1) * COLS, :], sem.at[step]
-            )
-
-        if load:
-            u_buf, v_buf, factor_sem = refs[5:]
-            copies = [
-                pltpu.make_async_copy(u_ref, u_buf, factor_sem.at[0]),
-                pltpu.make_async_copy(v_ref, v_buf, factor_sem.at[1]),
-            ]
-            for copy in copies:
-                copy.start()
-            u_ref, v_ref = u_buf, v_buf
+        sem, u_buf, v_buf, factor_sem = refs[4:]
+        copies = [
+            pltpu.make_async_copy(u_ref, u_buf, factor_sem.at[0]),
+            pltpu.make_async_copy(v_ref, v_buf, factor_sem.at[1]),
+        ]
+        for copy in copies:
+            copy.start()
         fetch(0).start()
         fetch(1).start()
-        if load:
-            for copy in copies:
-                copy.wait()
+        for copy in copies:
+            copy.wait()
         fetch(2).start()
+        u_ref, v_ref = u_buf, v_buf
     put_moving(u_ref, u_w, base if u_ref.shape[0] == RANK else None)
     sums = put_fixed(v_ref, v_t, v_cat)
     for step in range(steps):
         if first:
             fetch(step).wait()
+            fetch(step + 3).start()
         acc[:, step * COLS : (step + 1) * COLS] = slab(flow, True, v_t, v_cat, u_w, step)
     store_pieces(out_ref, acc, sums)
+    if first:
+        for step in range(steps, 2 * steps):
+            fetch(step).wait()
 
 
 def cost(zones_u, zones_v):
@@ -168,29 +170,28 @@
 
 def anchor_half(mine, flow, u, v, first=False):
     zones = flow.shape[1]
-    load = first and not mine
     out_shape = [jax.ShapeDtypeStruct((HALF_FORM[0] * PIECE, LANES), F32)]
     scratch = factor_scratch(HALF, zones)
-    in_specs = [VMEM] * 3
+    operands = [flow, u, v]
     if first:
-        out_shape.append(pltpu.VMEM((HALF, zones), F32))
-        scratch.append(pltpu.SemaphoreType.DMA((HALF // COLS,)))
-        in_specs[0] = ANY
-        flow = pltpu.with_memory_space_constraint(flow, pltpu.HBM)
-    if load:
-        in_specs = [ANY] * 3
-        u, v = (pltpu.with_memory_space_constraint(x, pltpu.HBM) for x in (u, v))
-        scratch += [pltpu.VMEM(u.shape, F32), pltpu.VMEM(v.shape, F32), pltpu.SemaphoreType.DMA((2,))]
+        out_shape += [pltpu.VMEM((HALF, zones), F32)] * 2
+        operands = [pltpu.with_memory_space_constraint(x, pltpu.HBM) for x in operands]
+        scratch += [
+            pltpu.SemaphoreType.DMA((2 * HALF // COLS,)),
+            pltpu.VMEM(u.shape, F32),
+            pltpu.VMEM(v.shape, F32),
+            pltpu.SemaphoreType.DMA((2,)),
+        ]
     return pl.pallas_call(
-        functools.partial(anchor_kernel, mine, first, load),
+        functools.partial(anchor_kernel, mine, first),
         out_shape=out_shape,
-        in_specs=in_specs,
+        in_specs=[ANY if first else VMEM] * 3,
         out_specs=[VMEM] * len(out_shape),
         scratch_shapes=scratch,
         cost_estimate=cost(HALF, zones),
         compiler_params=pltpu.CompilerParams(vmem_limit_bytes=24 * 2**20),
         name="anchor_mine" if mine else "anchor_other",
-    )(flow, u, v)
+    )(*operands)
 
 
 def near_kernel(flow, u_ref, v_ref, out_ref, v_t, v_cat, u_w):
@@ -200,20 +201,11 @@
         out_ref[:, step * COLS : (step + 1) * COLS] = slab(flow, False, v_t, v_cat, u_w, step)
 
 
-def far_kernel(emit, flow, u_ref, v_ref, near_ref, mine_ref, out_ref, *refs):
-    refs = list(refs)
-    v_out = refs.pop(0) if emit else None
-    v_t, v_cat, u_w, acc = refs
-    core = lax.rem(lax.axis_index("col"), 2)
+def far_kernel(flow, u_ref, v_ref, near_ref, mine_ref, out_ref, v_t, v_cat, u_w, acc):
     sums = put_fixed(v_ref, v_t, v_cat)
     for tile in range(HALF_FORM[2]):
         for part in range(3):
-            x = load_tile(mine_ref, part, tile)
-            sums[part] = sums[part] + x
-            if emit:
-                for y, owner in ((x, core), (load_tile(v_ref, part, tile), 1 - core)):
-                    at = pl.ds(pl.multiple_of(owner * HALF + tile * LANES, LANES), LANES)
-                    v_out[part * PART : (part + 1) * PART, at] = y
+            sums[part] = sums[part] + load_tile(mine_ref, part, tile)
     put_moving(u_ref, u_w)
     for step in range(u_w.shape[1] // COLS):
         at = slice(step * COLS, (step + 1) * COLS)
@@ -221,7 +213,7 @@
     store_pieces(out_ref, acc, sums)
 
 
-def destination_half(flow_mine, flow_other, u, mine, other, emit):
+def destination_half(flow_mine, flow_other, u, mine, other):
     zones = flow_mine.shape[1]
     params = dict(
         cost_estimate=cost(zones, HALF),
@@ -236,14 +228,11 @@
         name="destination_near",
         **params,
     )(flow_mine, u, mine)
-    out_shape = [jax.ShapeDtypeStruct((ROW_FORM[0] * PIECE, LANES), F32)]
-    if emit:
-        out_shape.append(jax.ShapeDtypeStruct((RANK, 2 * HALF), F32))
     return pl.pallas_call(
-        functools.partial(far_kernel, emit),
-        out_shape=out_shape,
+        far_kernel,
+        out_shape=jax.ShapeDtypeStruct((ROW_FORM[0] * PIECE, LANES), F32),
         in_specs=[VMEM] * 5,
-        out_specs=[VMEM] * len(out_shape),
+        out_specs=VMEM,
         scratch_shapes=factor_scratch(zones, HALF),
         name="destination_far",
         **params,
@@ -297,21 +286,28 @@
     )(got, old)
 
 
-def whole_kernel(in_ref, out_ref):
+def whole_kernel(mine_ref, other_ref, in_ref, anchor_out, destination_out):
+    core = lax.rem(lax.axis_index("col"), 2)
     for part in range(3):
+        ranks = slice(part * PART, (part + 1) * PART)
         for tile in range(ROW_FORM[2]):
-            out_ref[part * PART : (part + 1) * PART, lanes(tile)] = load_tile(in_ref, part, tile)
-
-
-def whole(pieces):
+            destination_out[ranks, lanes(tile)] = load_tile(in_ref, part, tile)
+        for ref, owner in ((mine_ref, core), (other_ref, 1 - core)):
+            for tile in range(HALF_FORM[2]):
+                at = pl.ds(pl.multiple_of(owner * HALF + tile * LANES, LANES), LANES)
+                anchor_out[ranks, at] = load_tile(ref, part, tile)
+
+
+def whole(mine, other, pieces):
+    shape = jax.ShapeDtypeStruct((RANK, 2 * HALF), F32)
     return pl.pallas_call(
         whole_kernel,
-        out_shape=jax.ShapeDtypeStruct((RANK, ROW_FORM[2] * LANES), F32),
-        in_specs=[VMEM],
-        out_specs=VMEM,
+        out_shape=[shape, shape],
+        in_specs=[VMEM] * 3,
+        out_specs=[VMEM] * 2,
         compiler_params=pltpu.CompilerParams(vmem_limit_bytes=4 * 2**20),
         name="whole",
-    )(pieces)
+    )(mine, other, pieces)
 
 
 def body(n_col, flow, anchor, destination):
@@ -329,17 +325,17 @@
 
     mine, other, flow_mine, flow_other = anchor, anchor, flow, flow
     for sweep in range(ITERS):
-        first, last = sweep == 0, sweep == ITERS - 1
+        first = sweep == 0
         sent, *rest = anchor_half(False, flow_other, other, destination, first)
-        flow_other = rest[0] if first else flow_other
+        if first:
+            flow_other, flow_mine = rest
         got = to_other(sent)
-        sent, *rest = anchor_half(True, flow_mine, mine, destination, first)
-        flow_mine = rest[0] if first else flow_mine
+        (sent,) = anchor_half(True, flow_mine, mine, destination)
         mine = over_chips(update("col", over_chips(sent + got), mine))
         other = to_other(mine)
-        sent, *rest = destination_half(flow_mine, flow_other, destination, mine, other, last)
+        sent = destination_half(flow_mine, flow_other, destination, mine, other)
         destination = over_row(update("row", over_row(sent), destination))
-    return rest[0], whole(destination)
+    return tuple(whole(mine, other, destination))
 
 
 def solution(mesh):

time: 131 us -> 130 us (level)
  Pallas kernels: 20.2 us -> 18.5 us
    pallas_call x7, Pallas kernels: 16.2 us -> 14.6 us  [the longest x4 10.2 us: anchor_half(): pl.pallas_call(functools.partial(anchor_kernel, mine, first), out_shape=o...]
  transfers between devices with their start and end apart: 4 -> 4, of which waited for: 0 -> 0; matrix products, arithmetic and copies ran while one was open for 0% -> 0% of each run, Pallas kernels for 7% -> 5%
where the time goes in v6:
time: 130 us; the launch traced here: 129 us
  blocking collectives  100 us (77%)
  Pallas kernels  18.5 us (14%)
  starting transfers between devices  9.94 us (8%)
    all_to_all x4, blocking collectives, over_chips(): return lax.all_to_all(x, 'col', 0, 0, axis_index_groups=cores, tiled=True)  50.3 us
    all_to_all x4, blocking collectives, over_row(): return lax.all_to_all(x, 'row', 0, 0, tiled=True)  49.7 us
    pallas_call x4, Pallas kernels, anchor_half(): pl.pallas_call(functools.partial(anchor_kernel, mine, first), out_shape=o...  10.2 us
    ppermute x4, starting transfers between devices, to_other(): return lax.ppermute(x, 'col', pairs)  9.94 us
    pallas_call x2, Pallas kernels, destination_half(): pl.pallas_call(far_kernel, out_shape=jax.ShapeDtypeStruct((ROW_FORM[0] *...  3.44 us
    pallas_call x2, Pallas kernels, destination_half(): pl.pallas_call(near_kernel, out_shape=jax.ShapeDtypeStruct((RANK, zones),...  3.34 us
  transfers between devices with their start and end apart: 4, of which 0 were waited for; matrix products, arithmetic and copies ran while one was open for 0% of the time, Pallas kernels for 5%

profile of v6, /device:TPU:1, one launch (start us, length us, event | category | flops | bytes accessed | tf_op | source)
XLA Modules:
  0.0 129.3 jit_solution(4503134487590363716)
XLA Ops:
  0.6 4.8 %anchor_other.2 = (f32[320,128]{1,0:T(8,128)S(1)}, f32[768,1536]{1,0:T(8,128)S(1)}, f32[768,1536]{1,0:T(8,128)S(1)}) custom-call(f32[1536,1536]{1,0:T(8,128)} %flow_in.1, f32[48,1536]{1,0:T(8,128)} %old_ref.2, f32[48,1536]{1,0:T(8,128)} %old_ref.3), custom_call_target="tpu_custom_call" | custom-call | flops 1179648000 | bytes 4718592 | tf_op jit(solution)/shard_map/anchor_other/pallas_call | solution.py:185
  5.5 3.3 %collective-permute-start = (f32[320,128]{1,0:T(8,128)S(1)}, f32[320,128]{1,0:T(8,128)S(1)}, u32[]{:S(2)}, u32[]{:S(2)}) collective-permute-start(f32[320,128]{1,0:T(8,128)S(1)} %get-tuple-element.6), channel_id=1, source_target_pairs={{0,1},{1,0},{2,3},{3,2},{4,5},{5,4},{6,7},{7,6},{8,9},{9,8},{10,11... | collective-permute-start | bytes 491528 | tf_op jit(solution)/shard_map/ppermute | solution.py:324
  8.8 1.8 %anchor_mine.2 = f32[320,128]{1,0:T(8,128)S(1)} custom-call(f32[768,1536]{1,0:T(8,128)S(1)} %get-tuple-element.5.flow_in.flow, f32[48,1536]{1,0:T(8,128)S(1)} %copy-done.1, f32[48,1536]{1,0:T(8,128)S(1)} %copy-done), custom_call_target="tpu_custom_call" | custom-call | flops 1179648000 | bytes 4718592 | tf_op jit(solution)/shard_map/anchor_mine/pallas_call | solution.py:185
  10.6 15.5 %all_to_all.88 = f32[8,40,128]{2,1,0:T(8,128)S(1)} all-to-all(f32[8,40,128]{2,1,0:T(8,128)S(1)} %bitcast.41), channel_id=1, replica_groups={{0,2,4,6,8,10,12,14},{1,3,5,7,9,11,13,15},{16,18,20,22,24,26,28,30},{17..., dimensions={0} | all-to-all | bytes 327680 | tf_op jit(solution)/shard_map/all_to_all | solution.py:321
  26.1 0.1 update.4
  26.2 10.8 %all_to_all.89 = f32[8,40,128]{2,1,0:T(8,128)S(1)} all-to-all(f32[8,40,128]{2,1,0:T(8,128)S(1)} %bitcast.40), channel_id=1, replica_groups={{0,2,4,6,8,10,12,14},{1,3,5,7,9,11,13,15},{16,18,20,22,24,26,28,30},{17..., dimensions={0} | all-to-all | bytes 327680 | tf_op jit(solution)/shard_map/all_to_all | solution.py:321
  37.0 2.6 %collective-permute-start.1 = (f32[320,128]{1,0:T(8,128)S(1)}, f32[320,128]{1,0:T(8,128)S(1)}, u32[]{:S(2)}, u32[]{:S(2)}) collective-permute-start(f32[320,128]{1,0:T(8,128)S(1)} %bitcast.21), channel_id=1, source_target_pairs={{0,1},{1,0},{2,3},{3,2},{4,5},{5,4},{6,7},{7,6},{8,9},{9,8},{10,11... | collective-permute-start | bytes 491528 | tf_op jit(solution)/shard_map/ppermute | solution.py:324
  39.6 1.7 %destination_near.2.near_ref = f32[48,1536]{1,0:T(8,128)S(1)} custom-call(f32[768,1536]{1,0:T(8,128)S(1)} %get-tuple-element.5.flow_in.flow, f32[48,1536]{1,0:T(8,128)S(1)} %copy-done, f32[320,128]{1,0:T(8,128)S(1)} %bitcast.22), custom_call_target="tpu_custom_call" | custom-call | flops 1179648000 | bytes 4718592 | tf_op jit(solution)/shard_map/destination_near/pallas_call | solution.py:222
  41.3 1.7 %destination_far.2 = f32[640,128]{1,0:T(8,128)S(1)} custom-call(f32[768,1536]{1,0:T(8,128)S(1)} %get-tuple-element.7.flow.flow_in, f32[48,1536]{1,0:T(8,128)S(1)} %copy-done, f32[320,128]{1,0:T(8,128)S(1)} %collective-permute-done.1.v_ref.u_ref, f32[48,1536]{1,0:T(8,128)S(1)} %destination_near.2.near_ref, f32[320,128]{1,0:T(8,128)S(1)} %bitcast.23), custom_call_target="tpu_custom_call" | custom-call | flops 1179648000 | bytes 4718592 | tf_op jit(solution)/shard_map/destination_far/pallas_call | solution.py:231
  43.0 15.6 %all_to_all.90 = f32[16,40,128]{2,1,0:T(8,128)S(1)} all-to-all(f32[16,40,128]{2,1,0:T(8,128)S(1)} %bitcast.31), channel_id=1, replica_groups=mesh['row'=16,'col'=16] {'row'}, dimensions={0} | all-to-all | bytes 655360 | tf_op jit(solution)/shard_map/all_to_all | solution.py:318
  58.6 0.2 update.5
  58.7 11.3 %all_to_all.91 = f32[16,40,128]{2,1,0:T(8,128)S(1)} all-to-all(f32[16,40,128]{2,1,0:T(8,128)S(1)} %bitcast.36), channel_id=1, replica_groups=mesh['row'=16,'col'=16] {'row'}, dimensions={0} | all-to-all | bytes 655360 | tf_op jit(solution)/shard_map/all_to_all | solution.py:318
  70.0 1.8 %anchor_other.3 = f32[320,128]{1,0:T(8,128)S(1)} custom-call(f32[768,1536]{1,0:T(8,128)S(1)} %get-tuple-element.7.flow.flow_in, f32[320,128]{1,0:T(8,128)S(1)} %collective-permute-done.1.v_ref.u_ref, f32[640,128]{1,0:T(8,128)S(1)} %bitcast.16), custom_call_target="tpu_custom_call" | custom-call | flops 1179648000 | bytes 4718592 | tf_op jit(solution)/shard_map/anchor_other/pallas_call | solution.py:185
  71.8 2.3 %collective-permute-start.2 = (f32[320,128]{1,0:T(8,128)S(1)}, f32[320,128]{1,0:T(8,128)S(1)}, u32[]{:S(2)}, u32[]{:S(2)}) collective-permute-start(f32[320,128]{1,0:T(8,128)S(1)} %anchor_other.3), channel_id=1, source_target_pairs={{0,1},{1,0},{2,3},{3,2},{4,5},{5,4},{6,7},{7,6},{8,9},{9,8},{10,11... | collective-permute-start | bytes 491528 | tf_op jit(solution)/shard_map/ppermute | solution.py:324
  74.1 1.8 %anchor_mine.3 = f32[320,128]{1,0:T(8,128)S(1)} custom-call(f32[768,1536]{1,0:T(8,128)S(1)} %get-tuple-element.5.flow_in.flow, f32[320,128]{1,0:T(8,128)S(1)} %bitcast.24, f32[640,128]{1,0:T(8,128)S(1)} %bitcast.17), custom_call_target="tpu_custom_call" | custom-call | flops 1179648000 | bytes 4718592 | tf_op jit(solution)/shard_map/anchor_mine/pallas_call | solution.py:185
  76.0 12.7 %all_to_all.92 = f32[8,40,128]{2,1,0:T(8,128)S(1)} all-to-all(f32[8,40,128]{2,1,0:T(8,128)S(1)} %bitcast.42), channel_id=1, replica_groups={{0,2,4,6,8,10,12,14},{1,3,5,7,9,11,13,15},{16,18,20,22,24,26,28,30},{17..., dimensions={0} | all-to-all | bytes 327680 | tf_op jit(solution)/shard_map/all_to_all | solution.py:321
  88.8 11.4 %all_to_all.93 = f32[8,40,128]{2,1,0:T(8,128)S(1)} all-to-all(f32[8,40,128]{2,1,0:T(8,128)S(1)} %bitcast.38), channel_id=1, replica_groups={{0,2,4,6,8,10,12,14},{1,3,5,7,9,11,13,15},{16,18,20,22,24,26,28,30},{17..., dimensions={0} | all-to-all | bytes 327680 | tf_op jit(solution)/shard_map/all_to_all | solution.py:321
  100.2 1.7 %collective-permute-start.3 = (f32[320,128]{1,0:T(8,128)S(1)}, f32[320,128]{1,0:T(8,128)S(1)}, u32[]{:S(2)}, u32[]{:S(2)}) collective-permute-start(f32[320,128]{1,0:T(8,128)S(1)} %bitcast.26), channel_id=1, source_target_pairs={{0,1},{1,0},{2,3},{3,2},{4,5},{5,4},{6,7},{7,6},{8,9},{9,8},{10,11... | collective-permute-start | bytes 491528 | tf_op jit(solution)/shard_map/ppermute | solution.py:324
  101.9 1.7 %destination_near.3.near_ref = f32[48,1536]{1,0:T(8,128)S(1)} custom-call(f32[768,1536]{1,0:T(8,128)S(1)} %get-tuple-element.5.flow_in.flow, f32[640,128]{1,0:T(8,128)S(1)} %bitcast.18, f32[320,128]{1,0:T(8,128)S(1)} %bitcast.27), custom_call_target="tpu_custom_call" | custom-call | flops 1179648000 | bytes 4718592 | tf_op jit(solution)/shard_map/destination_near/pallas_call | solution.py:222
  103.6 1.7 %destination_far.3 = f32[640,128]{1,0:T(8,128)S(1)} custom-call(f32[768,1536]{1,0:T(8,128)S(1)} %get-tuple-element.7.flow.flow_in, f32[640,128]{1,0:T(8,128)S(1)} %bitcast.19, f32[320,128]{1,0:T(8,128)S(1)} %collective-permute-done.3.v_ref.other_ref, f32[48,1536]{1,0:T(8,128)S(1)} %destination_near.3.near_ref, f32[320,128]{1,0:T(8,128)S(1)} %bitcast.28), custom_call_target="tpu_custom_call" | custom-call | flops 1179648000 | bytes 4718592 | tf_op jit(solution)/shard_map/destination_far/pallas_call | solution.py:231
  105.4 11.6 %all_to_all.94 = f32[16,40,128]{2,1,0:T(8,128)S(1)} all-to-all(f32[16,40,128]{2,1,0:T(8,128)S(1)} %bitcast.30), channel_id=1, replica_groups=mesh['row'=16,'col'=16] {'row'}, dimensions={0} | all-to-all | bytes 655360 | tf_op jit(solution)/shard_map/all_to_all | solution.py:318
  117.0 0.2 update.7
  117.1 11.3 %all_to_all.95 = f32[16,40,128]{2,1,0:T(8,128)S(1)} all-to-all(f32[16,40,128]{2,1,0:T(8,128)S(1)} %bitcast.34), channel_id=1, replica_groups=mesh['row'=16,'col'=16] {'row'}, dimensions={0} | all-to-all | bytes 655360 | tf_op jit(solution)/shard_map/all_to_all | solution.py:318
  128.4 0.9 whole.1
  (11 shorter events, 0.2 us)
Async XLA Ops:
  0.6 8.1 %copy-start = (f32[48,1536]{1,0:T(8,128)S(1)}, f32[48,1536]{1,0:T(8,128)}, u32[]{:S(2)}) copy-start(f32[48,1536]{1,0:T(8,128)} %old_ref.3) | copy-start | bytes 884740
  0.6 8.1 %copy-start.1 = (f32[48,1536]{1,0:T(8,128)S(1)}, f32[48,1536]{1,0:T(8,128)}, u32[]{:S(2)}) copy-start(f32[48,1536]{1,0:T(8,128)} %old_ref.2) | copy-start | bytes 884740
  5.5 5.1 %collective-permute-start = (f32[320,128]{1,0:T(8,128)S(1)}, f32[320,128]{1,0:T(8,128)S(1)}, u32[]{:S(2)}, u32[]{:S(2)}) collective-permute-start(f32[320,128]{1,0:T(8,128)S(1)} %get-tuple-element.6), channel_id=1, source_target_pairs={{0,1},{1,0},{2,3},{3,2},{4,5},{5,4},{6,7},{7,6},{8,9},{9,8},{10,11... | collective-permute-start | bytes 491528 | tf_op jit(solution)/shard_map/ppermute | solution.py:324
  37.0 4.3 %collective-permute-start.1 = (f32[320,128]{1,0:T(8,128)S(1)}, f32[320,128]{1,0:T(8,128)S(1)}, u32[]{:S(2)}, u32[]{:S(2)}) collective-permute-start(f32[320,128]{1,0:T(8,128)S(1)} %bitcast.21), channel_id=1, source_target_pairs={{0,1},{1,0},{2,3},{3,2},{4,5},{5,4},{6,7},{7,6},{8,9},{9,8},{10,11... | collective-permute-start | bytes 491528 | tf_op jit(solution)/shard_map/ppermute | solution.py:324
  71.8 4.2 %collective-permute-start.2 = (f32[320,128]{1,0:T(8,128)S(1)}, f32[320,128]{1,0:T(8,128)S(1)}, u32[]{:S(2)}, u32[]{:S(2)}) collective-permute-start(f32[320,128]{1,0:T(8,128)S(1)} %anchor_other.3), channel_id=1, source_target_pairs={{0,1},{1,0},{2,3},{3,2},{4,5},{5,4},{6,7},{7,6},{8,9},{9,8},{10,11... | collective-permute-start | bytes 491528 | tf_op jit(solution)/shard_map/ppermute | solution.py:324
  100.2 3.4 %collective-permute-start.3 = (f32[320,128]{1,0:T(8,128)S(1)}, f32[320,128]{1,0:T(8,128)S(1)}, u32[]{:S(2)}, u32[]{:S(2)}) collective-permute-start(f32[320,128]{1,0:T(8,128)S(1)} %bitcast.26), channel_id=1, source_target_pairs={{0,1},{1,0},{2,3},{3,2},{4,5},{5,4},{6,7},{7,6},{8,9},{9,8},{10,11... | collective-permute-start | bytes 491528 | tf_op jit(solution)/shard_map/ppermute | solution.py:324
